TPU v7x, 128 devices: a whole 4x4x4 slice. The times are simulated.
128 devices in a mesh: ctx: 8 (over y, core), exp: 16 (over z, x).
Axes of the slice: x: 4, y: 4, z: 4, core: 2. Of those that a mesh axis runs over, the one named last changes fastest.
Arguments:
- hidden: bfloat16 [16, 1024, 4096], P('exp', 'ctx'), may hold values from -6 to 6
- queries: bfloat16 [16, 1024, 4096], P('exp', 'ctx'), may hold values from -4.5 to 4.5
- new_keys: bfloat16 [16, 1024, 512], P('exp', 'ctx'), may hold values from -6 to 6
- new_values: bfloat16 [16, 1024, 512], P('exp', 'ctx'), may hold values from -6 to 6
- cache_keys: bfloat16 [16, 1024, 512], P('exp', 'ctx'), may hold values from -4.5 to 4.5
- cache_values: bfloat16 [16, 1024, 512], P('exp', 'ctx'), may hold values from -6 to 6
- out_weight: bfloat16 [4096, 4096], P(('ctx', 'exp')), may hold values from -1.5 to 1.5
- norm_gain: bfloat16 [4096], replicated, may hold values from 0.099609375 to 1.8984375
- gate_proj: bfloat16 [128, 4096, 768], P(('ctx', 'exp')), may hold values from -0.09375 to 0.09375
- up_proj: bfloat16 [128, 4096, 768], P(('ctx', 'exp')), may hold values from -0.09375 to 0.09375
- down_proj: bfloat16 [128, 768, 4096], P(('ctx', 'exp')), may hold values from -0.21875 to 0.21875
- expert_ids: int32 [16, 1024, 4], P('exp', 'ctx'), may hold values from 0 to 127, all different within a row; in each aligned block of 128 rows (0 to 127, 128 to 255, ..., all dimensions but the last counted through in order) at most 8 rows name the same one
- gate_fixed: int32 [16, 1024, 4], P('exp', 'ctx'), may hold values from 1 to 65535
Outputs:
- after_attention: bfloat16 [16, 1024, 4096], P('exp', 'ctx')
- layer_output: bfloat16 [16, 1024, 4096], P('exp', 'ctx')
Inputs may be any that keep to these rules, and one draw needn't show every extreme that they name: `expert_ids`: each row names 4 different experts. Within the rows of one device (aligned blocks of 128 rows, sequences taken in order) no expert is named more than 8 times, and in some blocks one expert is named exactly 8 times.
All inputs are finite; a program needn't handle non-finite values.
Results may differ from a plain program's by a relative error of at most 0.02.
Values may be sent and summed in bfloat16 or wider, within the bound.
A program may use at most 128 MiB of HBM per device.

v0:
```python
import math

import jax
import jax.numpy as jnp
from jax import lax
from jax.sharding import PartitionSpec as P

D = 4096
KVH = 4
HD = 128
TOPK = 4


def widen_heads(tensor, copies):
    row_count = tensor.shape[0]
    heads = tensor.reshape(row_count, KVH, HD)
    return jnp.repeat(heads, copies, axis=1).reshape(row_count, KVH * copies * HD)


def expert_ffn(incoming, gate_matrix, up_matrix, down_matrix):
    shape_in = incoming.shape
    flat_rows = incoming.reshape(-1, shape_in[-1])
    gate_act = jnp.dot(flat_rows, gate_matrix, preferred_element_type=jnp.float32)
    up_act = jnp.dot(flat_rows, up_matrix, preferred_element_type=jnp.float32)
    product = (jax.nn.silu(gate_act) * up_act).astype(jnp.bfloat16)
    output = jnp.dot(product, down_matrix, preferred_element_type=jnp.float32)
    return output.astype(jnp.bfloat16).reshape(shape_in)


def per_device(
    hidden,
    queries,
    new_keys,
    new_values,
    cache_keys,
    cache_values,
    out_weight,
    norm_gain,
    gate_proj,
    up_proj,
    down_proj,
    expert_ids,
    gate_fixed,
):
    context = lax.axis_size("ctx")
    experts_all = context * lax.axis_size("exp")
    tok_rows = hidden.shape[1]
    copies = context // KVH
    local_queries = queries[0]
    query_part, key_new, value_new, key_old, value_old = (
        lax.all_to_all(local_queries, "ctx", split_axis=1, concat_axis=0, tiled=True),
        lax.all_to_all(
            widen_heads(new_keys[0], copies), "ctx", split_axis=1, concat_axis=0, tiled=True
        ),
        lax.all_to_all(
            widen_heads(new_values[0], copies), "ctx", split_axis=1, concat_axis=0, tiled=True
        ),
        lax.all_to_all(
            widen_heads(cache_keys[0], copies), "ctx", split_axis=1, concat_axis=0, tiled=True
        ),
        lax.all_to_all(
            widen_heads(cache_values[0], copies), "ctx", split_axis=1, concat_axis=0, tiled=True
        ),
    )
    key_rows = jnp.concatenate([key_old, key_new], axis=0)
    value_rows = jnp.concatenate([value_old, value_new], axis=0)
    window = query_part.shape[0]
    heads_here = query_part.shape[1] // HD
    total_cache = key_old.shape[0]
    block_rows = min(512, window)
    block_count = window // block_rows
    key_pos = jnp.arange(key_rows.shape[0])

    def attend(operands):
        query_block, block_start = operands
        query_heads = query_block.reshape(block_rows, heads_here, HD)
        scores = jnp.einsum(
            "whd,ld->hwl", query_heads, key_rows, preferred_element_type=jnp.float32
        ) / math.sqrt(HD)
        query_pos = total_cache + block_start + jnp.arange(block_rows)
        scores = jnp.where(key_pos[None, None, :] <= query_pos[None, :, None], scores, -jnp.inf)
        highest = jnp.max(scores, axis=-1, keepdims=True)
        powers = jnp.exp(scores - highest)
        weights = (powers / jnp.sum(powers, axis=-1, keepdims=True)).astype(jnp.bfloat16)
        attended_block = jnp.einsum(
            "hwl,ld->whd", weights, value_rows, preferred_element_type=jnp.float32
        )
        return attended_block.astype(jnp.bfloat16).reshape(block_rows, heads_here * HD)

    attended = lax.map(
        attend,
        (
            query_part.reshape(block_count, block_rows, heads_here * HD),
            jnp.arange(block_count) * block_rows,
        ),
    ).reshape(window, heads_here * HD)
    proj_rows = lax.all_gather(out_weight, "exp", axis=0, tiled=True)
    projected = lax.psum_scatter(
        jnp.dot(attended, proj_rows, preferred_element_type=jnp.float32).astype(jnp.bfloat16),
        "ctx",
        scatter_dimension=0,
        tiled=True,
    ).astype(jnp.float32)
    after_attention = (hidden[0].astype(jnp.float32) + projected).astype(jnp.bfloat16)
    after_float = after_attention.astype(jnp.float32)
    normed = (
        after_float
        * lax.rsqrt(jnp.mean(after_float * after_float, axis=-1, keepdims=True) + 1e-06)
        * norm_gain.astype(jnp.float32)
    ).astype(jnp.bfloat16)
    capacity = max(2, 2 * tok_rows * TOPK // experts_all)
    flat_ids = expert_ids[0].reshape(-1)
    one_hot = (flat_ids[:, None] == jnp.arange(experts_all, dtype=jnp.int32)[None, :]).astype(
        jnp.int32
    )
    earlier = jnp.cumsum(one_hot, axis=0) - one_hot
    slot_index = jnp.sum(earlier * one_hot, axis=1)
    target = flat_ids * capacity + slot_index
    sources = jnp.repeat(normed, TOPK, axis=0)
    outgoing = jnp.zeros((experts_all * capacity, D), jnp.bfloat16).at[target].set(sources)
    results = expert_ffn(
        lax.all_to_all(
            outgoing.reshape(experts_all, capacity, D),
            ("ctx", "exp"),
            split_axis=0,
            concat_axis=0,
            tiled=True,
        ),
        gate_proj[0],
        up_proj[0],
        down_proj[0],
    )
    returned = lax.all_to_all(results, ("ctx", "exp"), split_axis=0, concat_axis=0, tiled=True)
    back_rows = returned.reshape(experts_all * capacity, D)[target]
    shares = gate_fixed[0].astype(jnp.float32) / 65536.0
    expert_sum = jnp.sum(
        back_rows.astype(jnp.float32).reshape(tok_rows, TOPK, D) * shares[:, :, None], axis=1
    )
    layer_output = (after_float + expert_sum).astype(jnp.bfloat16)
    return (after_attention[None], layer_output[None])


def solution(mesh):
    return jax.shard_map(
        per_device,
        mesh=mesh,
        in_specs=(
            P("exp", "ctx", None),
            P("exp", "ctx", None),
            P("exp", "ctx", None),
            P("exp", "ctx", None),
            P("exp", "ctx", None),
            P("exp", "ctx", None),
            P(("ctx", "exp"), None),
            P(),
            P(("ctx", "exp"), None, None),
            P(("ctx", "exp"), None, None),
            P(("ctx", "exp"), None, None),
            P("exp", "ctx", None),
            P("exp", "ctx", None),
        ),
        out_specs=(P("exp", "ctx", None), P("exp", "ctx", None)),
        check_vma=False,
    )
```

profile of v0, /device:TPU:12, one launch (start us, length us, event | category | flops | bytes accessed | tf_op | source)
XLA Modules:
  0.0 494.8 jit_solution(2503585815674640515)
XLA Ops:
  7.2 0.9 reshape_squeeze.14
  8.1 0.7 broadcast_in_dim.55
  8.9 4.9 all-to-all-start.2
  13.8 0.9 reshape_squeeze.13
  14.8 5.1 %all-to-all-done.2 = bf16[128,8,128]{2,0,1:T(8,128)(2,1)S(1)} async-done(((bf16[128,8,128]{2,0,1:T(8,128)(2,1)}), bf16[128,8,128]{2,0,1:T(8,128)(2,1)S(1)}, u32[]{:S(2)}, u32[]{:S(2)}) %all-to-all-start.2) | async-done | bytes 262176 | tf_op jit(solution)/shard_map/all_to_all | solution.py:52
  19.8 0.7 broadcast_in_dim.54
  20.6 4.8 all-to-all-start.1
  25.4 1.0 copy.96
  26.4 5.1 %all-to-all-done.1 = bf16[128,8,128]{2,0,1:T(8,128)(2,1)S(1)} async-done(((bf16[128,8,128]{2,0,1:T(8,128)(2,1)}), bf16[128,8,128]{2,0,1:T(8,128)(2,1)S(1)}, u32[]{:S(2)}, u32[]{:S(2)}) %all-to-all-start.1) | async-done | bytes 262176 | tf_op jit(solution)/shard_map/all_to_all | solution.py:58
  31.4 0.7 broadcast_in_dim.57
  32.2 4.8 all-to-all-start.4
  36.9 1.0 copy.95
  38.0 5.1 %all-to-all-done.4 = bf16[128,8,128]{0,2,1:T(8,128)(2,1)S(1)} async-done(((bf16[128,8,128]{0,2,1:T(8,128)(2,1)}), bf16[128,8,128]{0,2,1:T(8,128)(2,1)S(1)}, u32[]{:S(2)}, u32[]{:S(2)}) %all-to-all-start.4) | async-done | bytes 262176 | tf_op jit(solution)/shard_map/all_to_all | solution.py:55
  43.0 0.7 broadcast_in_dim.56
  43.8 4.8 all-to-all-start.3
  48.5 2.3 copy.77
  50.8 3.8 all-to-all-done.3
  54.6 4.9 all-to-all-start
  59.5 0.7 all-gather.2.cloned.1.call-update
  60.3 0.2 copy.84
  60.5 0.2 copy.82
  60.7 1.0 copy.86
  61.8 0.8 pad_maximum_fusion
  62.6 11.4 %all-to-all-done = bf16[128,8,512]{0,2,1:T(8,128)(2,1)S(1)} async-done(((bf16[128,8,512]{0,2,1:T(8,128)(2,1)}), bf16[128,8,512]{0,2,1:T(8,128)(2,1)S(1)}, u32[]{:S(2)}, u32[]{:S(2)}) %all-to-all-start) | async-done | bytes 1048608 | tf_op jit(solution)/shard_map/all_to_all | solution.py:51
  74.0 0.5 copy.78
  74.6 46.5 %while.11 = (s32[]{:T(128)}, bf16[2,512,512]{2,1,0:T(8,128)(2,1)}, s32[2]{0:T(128)S(1)}, bf16[2,512,512]{2,1,0:T(8,128)(2,1)S(1)}, bf16[2048,128]{1,0:T(8,128)(2...) while((s32[]{:T(128)}, bf16[2,512,512]{2,1,0:T(8,128)(2,1)}, s32[2]{0:T(128)S(1)}, ...), condition=%wide.region_3.4_spmd.clone, body=%wide.region_0.3_spmd.clone.sunk | while | flops 2173962752 | bytes 44060828 | solution.py:90
  74.6 0.6 dynamic_slice.14
  75.8 0.7 iota_compare_fusion.5
  76.5 0.2 copy.102
  76.8 11.0 %fusion.67 = (f32[4,512]{1,0:T(4,128)S(1)}, f32[4,512,2048]{2,1,0:T(8,128)}) fusion(pred[512,2048]{1,0:T(8,128)(4,1)S(1)} %iota_compare_fusion.5, bf16[512,4,128]{0,2,1:T(8,128)(2,1)S(1)} %bitcast.120, bf16[2048,128]{1,0:T(8,128)(2,1)} %get-tuple-element.155), kind=kOutput, calls=%fused_computation.67.clone.1 | convolution fusion | flops 1090521088 | bytes 18882560 | tf_op jit(solution)/shard_map/while/body/eval_jaxpr/sub | solution.py:83
  87.7 8.7 %fusion.68 = bf16[4,512,128]{1,2,0:T(8,128)(2,1)S(1)} fusion(f32[4,512,2048]{2,1,0:T(8,128)} %get-tuple-element.133, f32[4,512]{1,0:T(4,128)S(1)} %get-tuple-element.134, bf16[2048,128]{0,1:T(8,128)(2,1)S(1)} %copy-done.2), kind=kOutput, calls=%fused_computation.16.clone.1 | convolution fusion | flops 1082392576 | bytes 17833984 | tf_op jit(solution)/shard_map/while/body/eval_jaxpr/hwl,ld->whd/dot_general | solution.py:85
  96.5 0.2 copy.103
  96.7 0.8 constant_dynamic-update-slice_fusion.2
  97.5 0.6 dynamic_slice.14
  98.8 0.7 iota_compare_fusion.5
  99.5 0.2 copy.102
  99.7 11.0 %fusion.67 = (f32[4,512]{1,0:T(4,128)S(1)}, f32[4,512,2048]{2,1,0:T(8,128)}) fusion(pred[512,2048]{1,0:T(8,128)(4,1)S(1)} %iota_compare_fusion.5, bf16[512,4,128]{0,2,1:T(8,128)(2,1)S(1)} %bitcast.120, bf16[2048,128]{1,0:T(8,128)(2,1)} %get-tuple-element.155), kind=kOutput, calls=%fused_computation.67.clone.1 | convolution fusion | flops 1090521088 | bytes 18882560 | tf_op jit(solution)/shard_map/while/body/eval_jaxpr/sub | solution.py:83
  110.7 8.8 %fusion.68 = bf16[4,512,128]{1,2,0:T(8,128)(2,1)S(1)} fusion(f32[4,512,2048]{2,1,0:T(8,128)} %get-tuple-element.133, f32[4,512]{1,0:T(4,128)S(1)} %get-tuple-element.134, bf16[2048,128]{0,1:T(8,128)(2,1)S(1)} %copy-done.2), kind=kOutput, calls=%fused_computation.16.clone.1 | convolution fusion | flops 1082392576 | bytes 17833984 | tf_op jit(solution)/shard_map/while/body/eval_jaxpr/hwl,ld->whd/dot_general | solution.py:85
  119.5 0.2 copy.103
  119.8 0.8 constant_dynamic-update-slice_fusion.2
  121.1 10.3 %convolution_convert_fusion = bf16[1024,4096]{1,0:T(8,128)(2,1)} fusion(bf16[1024,512]{1,0:T(8,128)(2,1)} %bitcast.141, bf16[512,4096]{1,0:T(8,128)(2,1)} %all-gather.2.cloned.1.call-done), kind=kOutput, calls=%fused_computation.32 | convolution fusion | flops 4299161600 | bytes 13631488 | tf_op jit(solution)/shard_map/dot_general | solution.py:99
  131.4 0.7 copy-done.4
  132.0 0.1 copy.89
  132.4 0.1 copy.88
  132.6 0.1 copy.91
  132.7 0.2 fusion.45
  133.0 0.2 fusion.44
  133.3 49.6 %reduce-scatter.2.cloned.1.call-done = bf16[128,4096]{1,0:T(8,128)(2,1)} async-done(((bf16[1024,4096]{1,0:T(8,128)(2,1)}), bf16[128,4096]{1,0:T(8,128)(2,1)}) %reduce-scatter.2.cloned.1.call-update) | async-done | bytes 1048592 | tf_op jit(solution)/shard_map/reduce_scatter | solution.py:98
  182.9 1.7 fusion.37
  184.6 0.3 fusion.39
  185.0 4.1 broadcast_in_dim.60
  189.0 6.9 %reshape.184 = bf16[512,4096]{1,0:T(8,128)(2,1)} reshape(bf16[128,4,4096]{2,1,0:T(4,128)(2,1)} %broadcast_in_dim.60) | data formatting | bytes 8388608 | tf_op jit(solution)/shard_map/reshape | solution.py:119
  195.9 12.6 %scatter_custom_fusion = bf16[1024,4096]{1,0:T(8,128)(2,1)} fusion(s32[512]{0:T(512)S(1)} %bitcast.135, bf16[512,4096]{1,0:T(8,128)(2,1)} %reshape.184, bf16[]{:T(256)} %constant.25.clone.1), kind=kCustom, calls=%fused_computation.36 | custom fusion | bytes 8389120 | tf_op jit(solution)/shard_map/scatter | solution.py:120
  208.5 105.4 %all_to_all.102 = bf16[128,8,4096]{2,1,0:T(8,128)(2,1)S(1)} all-to-all(bf16[128,8,4096]{2,1,0:T(8,128)(2,1)} %bitcast.119), channel_id=1, replica_groups=mesh['ctx'=8,'exp'=16] {'ctx','exp'}, dimensions={0} | all-to-all | bytes 16777216 | tf_op jit(solution)/shard_map/all_to_all | solution.py:122
  314.0 9.2 %fusion.24 = f32[1024,768]{1,0:T(8,128)S(1)} fusion(bf16[128,8,4096]{2,1,0:T(8,128)(2,1)S(1)} %all_to_all.102, bf16[1,4096,768]{2,1,0:T(8,128)(2,1)} %param.24), kind=kOutput, calls=%fused_computation.26 | convolution fusion | flops 6442450944 | bytes 17825792 | tf_op jit(solution)/shard_map/dot_general | solution.py:24
  323.2 7.0 %multiply_convert_fusion = bf16[1024,768]{1,0:T(8,128)(2,1)S(1)} fusion(f32[1024,768]{1,0:T(8,128)S(1)} %fusion.24, bf16[1,4096,768]{2,1,0:T(8,128)(2,1)S(1)} %bitcast.138, bf16[128,8,4096]{2,1,0:T(8,128)(2,1)S(1)} %all_to_all.102), kind=kOutput, calls=%fused_computation.38 | convolution fusion | flops 6447169536 | bytes 19398656 | tf_op jit(solution)/shard_map/dot_general | solution.py:23
  330.2 8.8 %convert_bitcast_fusion = bf16[128,8,4096]{2,1,0:T(8,128)(2,1)} fusion(bf16[1024,768]{1,0:T(8,128)(2,1)S(1)} %multiply_convert_fusion, bf16[1,768,4096]{2,1,0:T(8,128)(2,1)S(1)} %bitcast.140), kind=kOutput, calls=%fused_computation.31 | convolution fusion | flops 6446645248 | bytes 16252928 | tf_op jit(solution)/shard_map/dot_general | solution.py:26
  339.0 7.3 %all-to-all-start.6 = ((bf16[128,8,4096]{2,1,0:T(8,128)(2,1)}), bf16[128,8,4096]{2,1,0:T(8,128)(2,1)}, u32[]{:S(2)}, u32[]{:S(2)}) async-start(bf16[128,8,4096]{2,1,0:T(8,128)(2,1)} %convert_bitcast_fusion), calls=%async_computation.7 | async-start | bytes 16777216 | tf_op jit(solution)/shard_map/all_to_all | solution.py:133
  346.4 0.1 copy.93
  346.5 108.7 %all-to-all-done.6 = bf16[128,8,4096]{2,1,0:T(8,128)(2,1)} async-done(((bf16[128,8,4096]{2,1,0:T(8,128)(2,1)}), bf16[128,8,4096]{2,1,0:T(8,128)(2,1)}, u32[]{:S(2)}, u32[]{:S(2)}) %all-to-all-start.6) | async-done | bytes 8388640 | tf_op jit(solution)/shard_map/all_to_all | solution.py:133
  455.2 13.1 %gather_fusion = bf16[512,4096]{1,0:T(8,128)(2,1)} fusion(bf16[1024,4096]{1,0:T(8,128)(2,1)} %bitcast.31, s32[1024]{0:T(1024)S(1)} %pad_clamp_fusion), kind=kCustom, calls=%fused_computation | custom fusion | bytes 8390656 | tf_op jit(solution)/shard_map/gather | solution.py:134
  468.3 8.3 %reshape.171 = f32[128,4,4096]{2,1,0:T(4,128)} reshape(bf16[512,4096]{1,0:T(8,128)(2,1)} %gather_fusion) | data formatting | bytes 12582912 | tf_op jit(solution)/shard_map/convert_element_type | solution.py:137
  476.6 9.8 %multiply_reduce_fusion = f32[128,4096]{1,0:T(8,128)S(1)} fusion(f32[128,4,4096]{2,1,0:T(4,128)} %reshape.171, f32[128,4]{1,0:T(8,128)S(1)} %copy.93), kind=kLoop, calls=%fused_computation.30 | loop fusion | flops 3670016 | bytes 10487808 | tf_op jit(solution)/shard_map/reduce_sum | solution.py:136
  486.3 1.2 fusion.42
  (51 shorter events, 0.7 us)
Async XLA Ops:
  8.9 11.0 %all-to-all-start.2 = ((bf16[128,8,128]{2,0,1:T(8,128)(2,1)}), bf16[128,8,128]{2,0,1:T(8,128)(2,1)S(1)}, u32[]{:S(2)}, u32[]{:S(2)}) async-start(bf16[128,8,128]{2,0,1:T(8,128)(2,1)} %bitcast.7), calls=%async_computation.2 | async-start | bytes 524288 | tf_op jit(solution)/shard_map/all_to_all | solution.py:52
  20.6 10.9 %all-to-all-start.1 = ((bf16[128,8,128]{2,0,1:T(8,128)(2,1)}), bf16[128,8,128]{2,0,1:T(8,128)(2,1)S(1)}, u32[]{:S(2)}, u32[]{:S(2)}) async-start(bf16[128,8,128]{2,0,1:T(8,128)(2,1)} %bitcast.4), calls=%async_computation.1 | async-start | bytes 524288 | tf_op jit(solution)/shard_map/all_to_all | solution.py:58
  32.2 10.9 %all-to-all-start.4 = ((bf16[128,8,128]{0,2,1:T(8,128)(2,1)}), bf16[128,8,128]{0,2,1:T(8,128)(2,1)S(1)}, u32[]{:S(2)}, u32[]{:S(2)}) async-start(bf16[128,8,128]{0,2,1:T(8,128)(2,1)} %bitcast.15), calls=%async_computation.4 | async-start | bytes 524288 | tf_op jit(solution)/shard_map/all_to_all | solution.py:55
  43.8 10.9 %all-to-all-start.3 = ((bf16[128,8,128]{0,2,1:T(8,128)(2,1)}), bf16[128,8,128]{0,2,1:T(8,128)(2,1)S(1)}, u32[]{:S(2)}, u32[]{:S(2)}) async-start(bf16[128,8,128]{0,2,1:T(8,128)(2,1)} %bitcast.11), calls=%async_computation.3 | async-start | bytes 524288 | tf_op jit(solution)/shard_map/all_to_all | solution.py:61
  54.6 19.4 %all-to-all-start = ((bf16[128,8,512]{0,2,1:T(8,128)(2,1)}), bf16[128,8,512]{0,2,1:T(8,128)(2,1)S(1)}, u32[]{:S(2)}, u32[]{:S(2)}) async-start(bf16[128,8,512]{0,2,1:T(8,128)(2,1)} %bitcast.1), calls=%async_computation | async-start | bytes 2097152 | tf_op jit(solution)/shard_map/all_to_all | solution.py:51
  59.5 61.5 %all-gather.2.cloned.1.call-start = ((), (), s32[]{:S(2)}) async-start(), calls=%async_computation.8 | async-start | bytes 4456448 | tf_op jit(solution)/shard_map/all_gather | solution.py:97
  60.3 122.7 %reduce-scatter.2.cloned.1.call-start = ((), (), s32[]{:S(2)}) async-start(), calls=%async_computation.9 | async-start | bytes 9437184 | tf_op jit(solution)/shard_map/reduce_scatter | solution.py:98
  76.8 11.0 %copy-start.2 = (bf16[2048,128]{0,1:T(8,128)(2,1)S(1)}, bf16[2048,128]{0,1:T(8,128)(2,1)}, u32[]{:S(2)}) copy-start(bf16[2048,128]{0,1:T(8,128)(2,1)} %get-tuple-element.156) | copy-start | bytes 1572868 | tf_op jit(solution)/shard_map/while
  99.7 11.0 %copy-start.2 = (bf16[2048,128]{0,1:T(8,128)(2,1)S(1)}, bf16[2048,128]{0,1:T(8,128)(2,1)}, u32[]{:S(2)}) copy-start(bf16[2048,128]{0,1:T(8,128)(2,1)} %get-tuple-element.156) | copy-start | bytes 1572868 | tf_op jit(solution)/shard_map/while
  131.3 0.7 copy-start.4
  131.3 1.7 copy-start.3
  131.3 51.6 %copy-start.1 = (bf16[1,128,4096]{2,1,0:T(8,128)(2,1)S(1)}, bf16[1,128,4096]{2,1,0:T(8,128)(2,1)}, u32[]{:S(2)}) copy-start(bf16[1,128,4096]{2,1,0:T(8,128)(2,1)} %param.15) | copy-start | bytes 3145732
  184.6 301.7 %copy-start = (bf16[128,4096]{1,0:T(8,128)(2,1)}, bf16[128,4096]{1,0:T(8,128)(2,1)S(1)}, u32[]{:S(2)}) copy-start(bf16[128,4096]{1,0:T(8,128)(2,1)S(1)} %get-tuple-element.91) | copy-start | bytes 3145732
  208.5 114.6 %slice-start = ((s8[6291456]{0:T(1024)(128)(4,1)}), s8[4194304]{0:T(1024)(128)(4,1)S(1)}, s32[]{:S(2)}) async-start(s8[6291456]{0:T(1024)(128)(4,1)} %bitcast.137), calls=%async_computation.10 | async-start | bytes 8388608
  314.0 9.2 %slice-start.1 = ((s8[6291456]{0:T(1024)(128)(4,1)}), s8[2097152]{0:T(1024)(128)(4,1)S(1)}, s32[]{:S(2)}) async-start(s8[6291456]{0:T(1024)(128)(4,1)} %bitcast.137), calls=%async_computation.11 | async-start | bytes 4194304
  314.0 16.2 %slice-start.2 = ((s8[6291456]{0:T(1024)(128)(4,1)}), s8[4194304]{0:T(1024)(128)(4,1)S(1)}, s32[]{:S(2)}) async-start(s8[6291456]{0:T(1024)(128)(4,1)} %bitcast.139), calls=%async_computation.12 | async-start | bytes 8388608
  323.2 7.0 %slice-start.3 = ((s8[6291456]{0:T(1024)(128)(4,1)}), s8[2097152]{0:T(1024)(128)(4,1)S(1)}, s32[]{:S(2)}) async-start(s8[6291456]{0:T(1024)(128)(4,1)} %bitcast.139), calls=%async_computation.13 | async-start | bytes 4194304
  339.0 7.4 %copy-start.5 = (s32[1,128,4]{1,2,0:T(4,128)S(1)}, s32[1,128,4]{1,2,0:T(4,128)}, u32[]{:S(2)}) copy-start(s32[1,128,4]{1,2,0:T(4,128)} %param.27) | copy-start | bytes 6148
  339.0 116.2 %all-to-all-start.6 = ((bf16[128,8,4096]{2,1,0:T(8,128)(2,1)}), bf16[128,8,4096]{2,1,0:T(8,128)(2,1)}, u32[]{:S(2)}, u32[]{:S(2)}) async-start(bf16[128,8,4096]{2,1,0:T(8,128)(2,1)} %convert_bitcast_fusion), calls=%async_computation.7 | async-start | bytes 16777216 | tf_op jit(solution)/shard_map/all_to_all | solution.py:133
Sparse Core Ops, SparseCore 0:
  62.5 53.6 all-gather.1
  131.5 51.3 reduce-scatter.1
where the time goes:
time: 503 us; the launch traced here: 495 us
  waiting for transfers between devices  190 us (38%)
  blocking collectives  105 us (21%)
  matrix products  74.7 us (15%)
  local copies, waits for them, and re-layouts  61.3 us (12%)
  starting transfers between devices  31.5 us (6%)
  other arithmetic  15.7 us (3%)
  between operations  14.8 us (3%)
    all_to_all x1, waiting for transfers between devices, per_device(): lax.all_to_all(results, ('ctx', 'exp'), split_axis=0, concat_axis=0, tile...  109 us
    all_to_all x1, blocking collectives, per_device(): lax.all_to_all(outgoing.reshape(experts_all, capacity, D), ('ctx', 'exp')...  105 us
    reduce_scatter x1, waiting for transfers between devices, per_device(): lax.psum_scatter(jnp.dot(attended, proj_rows, preferred_element_type=jnp....  49.6 us
    sub x2, matrix products, attend(): powers = jnp.exp(scores - highest)  21.9 us
    dot_general x2, matrix products, attend(): jnp.einsum('hwl,ld->whd', weights, value_rows, preferred_element_type=jnp...  17.6 us
    gather x1, local copies, waits for them, and re-layouts, per_device(): back_rows = returned.reshape(experts_all * capacity, D)[target]  13.1 us
    scatter x1, local copies, waits for them, and re-layouts, per_device(): jnp.zeros((experts_all * capacity, D), jnp.bfloat16).at[target].set(sources)  12.6 us
    all_to_all x1, waiting for transfers between devices, per_device(): lax.all_to_all(local_queries, 'ctx', split_axis=1, concat_axis=0, tiled=T...  11.4 us
  transfers between devices with their start and end apart: 8, of which 7 were waited for; matrix products, arithmetic and copies ran while one was open for 11% of the time, Pallas kernels for 0%

commit v1 on v0

v1 whole, which is shorter than its diff:
```python
import functools
import math

import jax
import jax.numpy as jnp
from jax import lax
from jax.experimental import pallas as pl
from jax.experimental.pallas import tpu as pltpu
from jax.sharding import PartitionSpec as P

D = 4096
KVH = 4
HD = 128
TOPK = 4
CAP = 8


def attention_kernel(blocks, heads, width, buf_ref, out_ref, keys, values):
    rows = buf_ref.shape[1]
    base = heads * HD
    span = blocks * rows

    def load(j, _):
        at = pl.multiple_of(j * rows, rows)
        keys[pl.ds(at, rows), :] = buf_ref[j, :, base : base + HD]
        keys[pl.ds(span + at, rows), :] = buf_ref[j, :, base + HD : base + 2 * HD]
        values[pl.ds(at, rows), :HD] = buf_ref[j, :, base + 2 * HD : base + 3 * HD]
        values[pl.ds(span + at, rows), :HD] = buf_ref[j, :, base + 3 * HD : base + 4 * HD]
        return 0

    lax.fori_loop(0, blocks, load, 0)
    values[:, HD:] = jnp.ones((2 * span, HD), jnp.bfloat16)
    scale = math.log2(math.e) / math.sqrt(HD)
    many = heads * rows

    def block(i, _):
        query = jnp.concatenate(
            [buf_ref[i, :, h * HD : (h + 1) * HD] for h in range(heads)], axis=0
        )
        chunks = span // width + (i * rows) // width + 1

        def chunk(k, carry, masked):
            best, total = carry
            at = pl.multiple_of(k * width, width)
            scores = lax.dot_general(
                query,
                keys[pl.ds(at, width), :],
                (((1,), (1,)), ((), ())),
                preferred_element_type=jnp.float32,
            )
            if masked:
                row = lax.broadcasted_iota(jnp.int32, (many, width), 0) % rows
                col = lax.broadcasted_iota(jnp.int32, (many, width), 1)
                scores = jnp.where(at + col <= span + i * rows + row, scores, -1e30)
            highest = jnp.maximum(best, jnp.max(scores, axis=1, keepdims=True))
            powers = jnp.exp2((scores - highest) * scale).astype(jnp.bfloat16)
            fade = jnp.exp2((best - highest) * scale)
            total = total * fade + jnp.dot(
                powers, values[pl.ds(at, width), :], preferred_element_type=jnp.float32
            )
            return highest, total

        carry = (jnp.full((many, 1), -1e30, jnp.float32), jnp.zeros((many, 2 * HD), jnp.float32))
        carry = lax.fori_loop(0, chunks - 1, functools.partial(chunk, masked=False), carry)
        _, total = chunk(chunks - 1, carry, True)
        result = (total[:, :HD] / total[:, HD:]).astype(jnp.bfloat16)
        at = pl.multiple_of(i * rows, rows)
        for h in range(heads):
            out_ref[pl.ds(at, rows), h * HD : (h + 1) * HD] = result[h * rows : (h + 1) * rows]
        return 0

    lax.fori_loop(0, blocks, block, 0)


def attention(buf, heads):
    blocks, rows, _ = buf.shape
    return pl.pallas_call(
        functools.partial(attention_kernel, blocks, heads, min(512, blocks * rows)),
        out_shape=jax.ShapeDtypeStruct((blocks * rows, heads * HD), jnp.bfloat16),
        in_specs=[pl.BlockSpec(memory_space=pltpu.VMEM)],
        out_specs=pl.BlockSpec(memory_space=pltpu.VMEM),
        scratch_shapes=[
            pltpu.VMEM((2 * blocks * rows, HD), jnp.bfloat16),
            pltpu.VMEM((2 * blocks * rows, 2 * HD), jnp.bfloat16),
        ],
        compiler_params=pltpu.CompilerParams(vmem_limit_bytes=32 * 2**20),
        name="attention",
    )(buf)


def per_device(
    hidden,
    queries,
    new_keys,
    new_values,
    cache_keys,
    cache_values,
    out_weight,
    norm_gain,
    gate_proj,
    up_proj,
    down_proj,
    expert_ids,
    gate_fixed,
):
    context = lax.axis_size("ctx")
    experts = context * lax.axis_size("exp")
    rows = hidden.shape[1]
    copies = context // KVH
    heads = queries.shape[2] // HD // context

    def split(array, parts):
        return jnp.swapaxes(array.reshape(rows, parts, -1), 0, 1)

    kv = jnp.concatenate(
        [split(a[0], KVH) for a in (cache_keys, new_keys, cache_values, new_values)], axis=2
    )
    packed = jnp.concatenate([split(queries[0], context), jnp.repeat(kv, copies, axis=0)], axis=2)
    received = lax.all_to_all(packed, "ctx", split_axis=0, concat_axis=0, tiled=True)
    attended = attention(received, heads)
    proj_rows = lax.all_gather(out_weight, "exp", axis=0, tiled=True)
    projected = lax.psum_scatter(
        jnp.dot(attended, proj_rows, preferred_element_type=jnp.float32).astype(jnp.bfloat16),
        "ctx",
        scatter_dimension=0,
        tiled=True,
    ).astype(jnp.float32)
    after_attention = (hidden[0].astype(jnp.float32) + projected).astype(jnp.bfloat16)
    after_float = after_attention.astype(jnp.float32)
    normed = (
        after_float
        * lax.rsqrt(jnp.mean(after_float * after_float, axis=-1, keepdims=True) + 1e-06)
        * norm_gain.astype(jnp.float32)
    ).astype(jnp.bfloat16)

    flat_ids = expert_ids[0].reshape(-1)
    one_hot = (flat_ids[:, None] == jnp.arange(experts, dtype=jnp.int32)[None, :]).astype(jnp.int32)
    earlier = jnp.cumsum(one_hot, axis=0) - one_hot
    target = flat_ids * CAP + jnp.sum(earlier * one_hot, axis=1)
    slots = experts * CAP
    hits = target.reshape(rows, TOPK)[:, :, None] == jnp.arange(slots, dtype=jnp.int32)
    shares = gate_fixed[0][:, :, None]
    high = jnp.sum(jnp.where(hits, shares // 256, 0), axis=1).astype(jnp.bfloat16)
    low = jnp.sum(jnp.where(hits, shares % 256, 0), axis=1).astype(jnp.bfloat16)
    pick = jnp.any(hits, axis=1).astype(jnp.bfloat16)

    half = D // 2
    exchange = functools.partial(
        lax.all_to_all, axis_name=("ctx", "exp"), split_axis=0, concat_axis=0, tiled=True
    )

    def send(columns):
        rows_out = lax.dot_general(
            pick, columns, (((0,), (0,)), ((), ())), preferred_element_type=jnp.float32
        ).astype(jnp.bfloat16)
        return exchange(rows_out.reshape(experts, CAP, half)).reshape(slots, half)

    first, second = send(normed[:, :half]), send(normed[:, half:])

    def hidden_units(weight):
        return jnp.dot(first, weight[:half], preferred_element_type=jnp.float32) + jnp.dot(
            second, weight[half:], preferred_element_type=jnp.float32
        )

    act = (jax.nn.silu(hidden_units(gate_proj[0])) * hidden_units(up_proj[0])).astype(jnp.bfloat16)

    def give_back(weight):
        out = jnp.dot(act, weight, preferred_element_type=jnp.float32).astype(jnp.bfloat16)
        back = exchange(out.reshape(experts, CAP, half)).reshape(slots, half)
        return jnp.dot(high, back, preferred_element_type=jnp.float32) * (1 / 256) + jnp.dot(
            low, back, preferred_element_type=jnp.float32
        ) * (1 / 65536)

    expert_sum = jnp.concatenate(
        [give_back(down_proj[0][:, :half]), give_back(down_proj[0][:, half:])], axis=1
    )
    layer_output = (after_float + expert_sum).astype(jnp.bfloat16)
    return (after_attention[None], layer_output[None])


def solution(mesh):
    tokens = P("exp", "ctx", None)
    experts = P(("ctx", "exp"), None, None)
    return jax.shard_map(
        per_device,
        mesh=mesh,
        in_specs=(tokens,) * 6
        + (P(("ctx", "exp"), None), P(), experts, experts, experts, tokens, tokens),
        out_specs=(tokens, tokens),
        check_vma=False,
    )
```

time: 503 us -> 405 us (0.81); the launches traced: 495 us -> 402 us
  blocking collectives: 105 us -> 30.7 us
  local copies, waits for them, and re-layouts: 61.3 us -> 7.65 us
  waiting for transfers between devices: 190 us -> 218 us
  Pallas kernels: 0 us -> 25 us
  other arithmetic: 15.7 us -> 5.17 us
    all_to_all x1, blocking collectives: 105 us -> 30.7 us  [per_device(): lax.all_to_all(packed, 'ctx', split_axis=0, concat_axis=0, tiled=True)]
    all_to_all x6 -> x4, waiting for transfers between devices: 139 us -> 168 us  [the longest x2 88.5 us: give_back(): back = exchange(out.reshape(experts, CAP, half)).reshape(slots, half)]
    pallas_call x0 -> x1, Pallas kernels: none -> 25 us  [attention(): pl.pallas_call(functools.partial(attention_kernel, blocks, heads, min(512...]
    sub x2 -> x0, matrix products: 21.9 us -> none  [attend(): powers = jnp.exp(scores - highest)]
    dot_general x5 -> x12, matrix products: 42.5 us -> 61 us  [the longest x2 16.5 us: hidden_units(): jnp.dot(second, weight[half:], preferred_element_type=jnp.float32)]
    gather x1 -> x0, local copies, waits for them, and re-layouts: 13.1 us -> none  [per_device(): back_rows = returned.reshape(experts_all * capacity, D)[target]]
    scatter x1 -> x0, local copies, waits for them, and re-layouts: 12.6 us -> none  [per_device(): jnp.zeros((experts_all * capacity, D), jnp.bfloat16).at[target].set(sources)]
    reduce_sum x2, other arithmetic: 9.98 us -> 0.67 us  [the longest x1 0.44 us: per_device(): jnp.sum(jnp.where(hits, shares // 256, 0), axis=1).astype(jnp.bfloat16)]
  transfers between devices with their start and end apart: 8 -> 6, of which waited for: 7 -> 5; matrix products, arithmetic and copies ran while one was open for 11% -> 9% of each run, Pallas kernels for 0% -> 6%
where the time goes in v1:
time: 405 us; the launch traced here: 402 us
  waiting for transfers between devices  218 us (54%)
  matrix products  69.9 us (17%)
  starting transfers between devices  31 us (8%)
  blocking collectives  30.7 us (8%)
  Pallas kernels  25 us (6%)
  between operations  14.4 us (4%)
  local copies, waits for them, and re-layouts  7.65 us (2%)
  other arithmetic  5.17 us (1%)
    all_to_all x2, waiting for transfers between devices, give_back(): back = exchange(out.reshape(experts, CAP, half)).reshape(slots, half)  88.5 us
    all_to_all x2, waiting for transfers between devices, send(): return exchange(rows_out.reshape(experts, CAP, half)).reshape(slots, half)  79.9 us
    reduce_scatter x1, waiting for transfers between devices, per_device(): lax.psum_scatter(jnp.dot(attended, proj_rows, preferred_element_type=jnp....  49.2 us
    all_to_all x1, blocking collectives, per_device(): lax.all_to_all(packed, 'ctx', split_axis=0, concat_axis=0, tiled=True)  30.7 us
    pallas_call x1, Pallas kernels, attention(): pl.pallas_call(functools.partial(attention_kernel, blocks, heads, min(512...  25 us
    all_to_all x2, starting transfers between devices, send(): return exchange(rows_out.reshape(experts, CAP, half)).reshape(slots, half)  17.2 us
    dot_general x2, matrix products, hidden_units(): jnp.dot(second, weight[half:], preferred_element_type=jnp.float32)  16.5 us
    all_to_all x2, starting transfers between devices, give_back(): back = exchange(out.reshape(experts, CAP, half)).reshape(slots, half)  13.7 us
  transfers between devices with their start and end apart: 6, of which 5 were waited for; matrix products, arithmetic and copies ran while one was open for 9% of the time, Pallas kernels for 6%

profile of v1, /device:TPU:12, one launch (start us, length us, event | category | flops | bytes accessed | tf_op | source)
XLA Modules:
  0.0 402.2 jit_solution(6091756450250080618)
XLA Ops:
  7.2 0.0 copy-start.1
  7.2 0.0 all-gather.2.cloned.1.call-start
  7.2 0.7 all-gather.2.cloned.1.call-update
  7.9 0.0 reduce-scatter.2.cloned.1.call-start
  8.0 0.9 reshape_squeeze.17
  8.9 0.9 reshape_squeeze.18
  9.8 0.9 reshape_squeeze.19
  10.8 0.9 reshape_squeeze.20
  11.7 0.3 pad_maximum_fusion.1
  12.0 0.1 copy.31
  12.1 0.0 copy-done.1
  12.2 0.7 copy.29
  12.8 0.5 copy.30
  13.4 0.1 broadcast_in_dim.31
  13.5 0.3 pad_maximum_fusion
  13.7 30.7 %all_to_all.25.buf_ref = bf16[8,128,1024]{2,1,0:T(8,128)(2,1)S(1)} all-to-all(bf16[8,128,1024]{2,1,0:T(8,128)(2,1)S(1)} %pad_maximum_fusion), channel_id=1, replica_groups=mesh['ctx'=8,'exp'=16] {'ctx'}, dimensions={0} | all-to-all | bytes 4194304 | tf_op jit(solution)/shard_map/all_to_all | solution.py:119
  44.4 25.0 %attention.1 = bf16[1024,512]{1,0:T(8,128)(2,1)S(1)} custom-call(bf16[8,128,1024]{2,1,0:T(8,128)(2,1)S(1)} %all_to_all.25.buf_ref), custom_call_target="tpu_custom_call" | custom-call | tf_op jit(solution)/shard_map/attention/pallas_call | solution.py:77
  69.5 0.0 all-gather.2.cloned.1.call-done
  69.5 8.9 %convolution_convert_fusion = bf16[1024,4096]{1,0:T(8,128)(2,1)} fusion(bf16[1024,512]{1,0:T(8,128)(2,1)S(1)} %attention.1, bf16[512,4096]{1,0:T(8,128)(2,1)} %all-gather.2.cloned.1.call-done), kind=kOutput, calls=%fused_computation | convolution fusion | flops 4299161600 | bytes 13631488 | tf_op jit(solution)/shard_map/dot_general | solution.py:123
  78.4 0.0 reduce-scatter.2.cloned.1.call-update
  78.4 0.7 copy-done.4
  79.1 0.1 copy.32
  79.2 0.1 eq.44
  79.3 0.1 eq.40
  79.4 0.1 copy.35
  79.5 0.2 fusion.59
  79.9 0.2 fusion.58
  80.1 0.1 reduce_sum.39
  80.2 0.1 copy.37
  80.3 0.0 copy-done.3
  80.3 0.4 fusion.49
  80.7 49.2 %reduce-scatter.2.cloned.1.call-done = bf16[128,4096]{1,0:T(8,128)(2,1)} async-done(((bf16[1024,4096]{1,0:T(8,128)(2,1)}), bf16[128,4096]{1,0:T(8,128)(2,1)}) %reduce-scatter.2.cloned.1.call-update) | async-done | bytes 1048592 | tf_op jit(solution)/shard_map/reduce_scatter | solution.py:122
  129.9 0.0 copy-done.2
  129.9 1.7 fusion.44
  131.6 0.0 copy-start
  131.6 0.3 fusion.46
  131.9 3.2 convert_bitcast_fusion.2
  135.2 10.3 %all-to-all-start.2 = ((bf16[128,8,2048]{2,1,0:T(8,128)(2,1)}), bf16[128,8,2048]{2,1,0:T(8,128)(2,1)}, u32[]{:S(2)}, u32[]{:S(2)}) async-start(bf16[128,8,2048]{2,1,0:T(8,128)(2,1)} %convert_bitcast_fusion.2), calls=%async_computation.3 | async-start | bytes 8388608 | tf_op jit(solution)/shard_map/all_to_all | solution.py:156
  145.5 3.3 convert_bitcast_fusion.3
  148.8 46.6 %all-to-all-done.2 = bf16[128,8,2048]{2,1,0:T(8,128)(2,1)} async-done(((bf16[128,8,2048]{2,1,0:T(8,128)(2,1)}), bf16[128,8,2048]{2,1,0:T(8,128)(2,1)}, u32[]{:S(2)}, u32[]{:S(2)}) %all-to-all-start.2) | async-done | bytes 4194336 | tf_op jit(solution)/shard_map/all_to_all | solution.py:156
  195.3 6.9 %all-to-all-start.1 = ((bf16[128,8,2048]{2,1,0:T(8,128)(2,1)}), bf16[128,8,2048]{2,1,0:T(8,128)(2,1)}, u32[]{:S(2)}, u32[]{:S(2)}) async-start(bf16[128,8,2048]{2,1,0:T(8,128)(2,1)} %convert_bitcast_fusion.3), calls=%async_computation.2 | async-start | bytes 8388608 | tf_op jit(solution)/shard_map/all_to_all | solution.py:156
  202.2 8.2 %fusion.10 = f32[1024,768]{1,0:T(8,128)} fusion(bf16[128,8,2048]{2,1,0:T(8,128)(2,1)} %all-to-all-done.2, bf16[1,4096,768]{2,1,0:T(8,128)(2,1)} %param.21), kind=kOutput, calls=%fused_computation.11 | convolution fusion | flops 3221225472 | bytes 10485760 | tf_op jit(solution)/shard_map/dot_general | solution.py:161
  210.5 8.2 %fusion.8 = f32[1024,768]{1,0:T(8,128)} fusion(bf16[128,8,2048]{2,1,0:T(8,128)(2,1)} %all-to-all-done.2, bf16[1,4096,768]{2,1,0:T(8,128)(2,1)} %param.22), kind=kOutput, calls=%fused_computation.9 | convolution fusion | flops 3221225472 | bytes 10485760 | tf_op jit(solution)/shard_map/dot_general | solution.py:161
  218.7 33.4 %all-to-all-done.1 = bf16[128,8,2048]{2,1,0:T(8,128)(2,1)} async-done(((bf16[128,8,2048]{2,1,0:T(8,128)(2,1)}), bf16[128,8,2048]{2,1,0:T(8,128)(2,1)}, u32[]{:S(2)}, u32[]{:S(2)}) %all-to-all-start.1) | async-done | bytes 4194336 | tf_op jit(solution)/shard_map/all_to_all | solution.py:156
  252.1 6.3 %fusion.12 = f32[1024,768]{1,0:T(8,128)S(1)} fusion(bf16[128,8,2048]{2,1,0:T(8,128)(2,1)} %all-to-all-done.1, bf16[1,4096,768]{2,1,0:T(8,128)(2,1)} %param.22), kind=kOutput, calls=%fused_computation.13 | convolution fusion | flops 3221225472 | bytes 10485760 | tf_op jit(solution)/shard_map/dot_general | solution.py:161
  258.3 0.0 copy-done.6
  258.4 0.0 copy-done.7
  258.4 0.0 slice-start.1
  258.4 7.2 %multiply_convert_fusion = bf16[1024,768]{1,0:T(8,128)(2,1)S(1)} fusion(f32[1024,768]{1,0:T(8,128)S(1)} %fusion.12, f32[1024,768]{1,0:T(8,128)S(1)} %copy-done.7, f32[1024,768]{1,0:T(8,128)S(1)} %copy-done.6, bf16[1,4096,768]{2,1,0:T(8,128)(2,1)} %param.21, bf16[128,8,2048]{2,1,0:T(8,128)(2,1)} %all-to-all-done.1), kind=kOutput, calls=%fused_computation.27 | convolution fusion | flops 3227516928 | bytes 18350080 | tf_op jit(solution)/shard_map/dot_general | solution.py:161
  265.6 1.2 copy-done.8
  266.8 0.0 slice-done
  266.8 5.0 %convert_bitcast_fusion.1 = bf16[128,8,2048]{2,1,0:T(8,128)(2,1)} fusion(bf16[1024,768]{1,0:T(8,128)(2,1)S(1)} %multiply_convert_fusion, bf16[768,4096]{1,0:T(8,128)(2,1)S(1)} %bitcast.128), kind=kOutput, calls=%fused_computation.18 | convolution fusion | flops 3223322624 | bytes 8912896 | tf_op jit(solution)/shard_map/dot_general | solution.py:168
  271.8 6.9 %all-to-all-start.3 = ((bf16[128,8,2048]{2,1,0:T(8,128)(2,1)}), bf16[128,8,2048]{2,1,0:T(8,128)(2,1)}, u32[]{:S(2)}, u32[]{:S(2)}) async-start(bf16[128,8,2048]{2,1,0:T(8,128)(2,1)} %convert_bitcast_fusion.1), calls=%async_computation.4 | async-start | bytes 8388608 | tf_op jit(solution)/shard_map/all_to_all | solution.py:169
  278.7 7.8 %convert_bitcast_fusion = bf16[128,8,2048]{2,1,0:T(8,128)(2,1)} fusion(bf16[1024,768]{1,0:T(8,128)(2,1)} %copy-done.8, bf16[768,4096]{1,0:T(8,128)(2,1)} %bitcast.125), kind=kOutput, calls=%fused_computation.17 | convolution fusion | flops 3223322624 | bytes 8912896 | tf_op jit(solution)/shard_map/dot_general | solution.py:168
  286.5 42.1 %all-to-all-done.3 = bf16[128,8,2048]{2,1,0:T(8,128)(2,1)} async-done(((bf16[128,8,2048]{2,1,0:T(8,128)(2,1)}), bf16[128,8,2048]{2,1,0:T(8,128)(2,1)}, u32[]{:S(2)}, u32[]{:S(2)}) %all-to-all-start.3) | async-done | bytes 4194336 | tf_op jit(solution)/shard_map/all_to_all | solution.py:169
  328.5 6.9 %all-to-all-start.4 = ((bf16[128,8,2048]{2,1,0:T(8,128)(2,1)}), bf16[128,8,2048]{2,1,0:T(8,128)(2,1)}, u32[]{:S(2)}, u32[]{:S(2)}) async-start(bf16[128,8,2048]{2,1,0:T(8,128)(2,1)} %convert_bitcast_fusion), calls=%async_computation.5 | async-start | bytes 8388608 | tf_op jit(solution)/shard_map/all_to_all | solution.py:169
  335.4 0.0 copy-done.5
  335.4 0.4 select_reduce_fusion.1
  335.9 2.9 fusion.32
  338.8 46.5 %all-to-all-done.4 = bf16[128,8,2048]{2,1,0:T(8,128)(2,1)} async-done(((bf16[128,8,2048]{2,1,0:T(8,128)(2,1)}), bf16[128,8,2048]{2,1,0:T(8,128)(2,1)}, u32[]{:S(2)}, u32[]{:S(2)}) %all-to-all-start.4) | async-done | bytes 4194336 | tf_op jit(solution)/shard_map/all_to_all | solution.py:169
  385.3 2.9 fusion.41
  388.2 2.9 fusion.29
  391.1 3.0 fusion.38
  394.1 1.2 fusion.54
  (21 shorter events, 0.1 us)
Async XLA Ops:
  7.2 5.0 %copy-start.1 = (bf16[1,128,4096]{2,1,0:T(8,128)(2,1)S(1)}, bf16[1,128,4096]{2,1,0:T(8,128)(2,1)}, u32[]{:S(2)}) copy-start(bf16[1,128,4096]{2,1,0:T(8,128)(2,1)} %param.14) | copy-start | bytes 3145732
  7.2 62.3 %all-gather.2.cloned.1.call-start = ((), (), s32[]{:S(2)}) async-start(), calls=%async_computation.6 | async-start | bytes 4456448 | tf_op jit(solution)/shard_map/all_gather | solution.py:121
  7.9 122.0 %reduce-scatter.2.cloned.1.call-start = ((), (), s32[]{:S(2)}) async-start(), calls=%async_computation.7 | async-start | bytes 9437184 | tf_op jit(solution)/shard_map/reduce_scatter | solution.py:122
  78.4 0.7 copy-start.4
  78.4 1.9 copy-start.3
  79.1 50.8 %copy-start.2 = (bf16[1,128,4096]{2,1,0:T(8,128)(2,1)S(1)}, bf16[1,128,4096]{2,1,0:T(8,128)(2,1)}, u32[]{:S(2)}) copy-start(bf16[1,128,4096]{2,1,0:T(8,128)(2,1)} %param.13) | copy-start | bytes 3145732
  131.6 262.5 %copy-start = (bf16[128,4096]{1,0:T(8,128)(2,1)}, bf16[128,4096]{1,0:T(8,128)(2,1)S(1)}, u32[]{:S(2)}) copy-start(bf16[128,4096]{1,0:T(8,128)(2,1)S(1)} %get-tuple-element.5) | copy-start | bytes 3145732
  135.2 60.2 %all-to-all-start.2 = ((bf16[128,8,2048]{2,1,0:T(8,128)(2,1)}), bf16[128,8,2048]{2,1,0:T(8,128)(2,1)}, u32[]{:S(2)}, u32[]{:S(2)}) async-start(bf16[128,8,2048]{2,1,0:T(8,128)(2,1)} %convert_bitcast_fusion.2), calls=%async_computation.3 | async-start | bytes 8388608 | tf_op jit(solution)/shard_map/all_to_all | solution.py:156
  195.3 56.7 %all-to-all-start.1 = ((bf16[128,8,2048]{2,1,0:T(8,128)(2,1)}), bf16[128,8,2048]{2,1,0:T(8,128)(2,1)}, u32[]{:S(2)}, u32[]{:S(2)}) async-start(bf16[128,8,2048]{2,1,0:T(8,128)(2,1)} %convert_bitcast_fusion.3), calls=%async_computation.2 | async-start | bytes 8388608 | tf_op jit(solution)/shard_map/all_to_all | solution.py:156
  252.1 6.3 %copy-start.6 = (f32[1024,768]{1,0:T(8,128)S(1)}, f32[1024,768]{1,0:T(8,128)}, u32[]{:S(2)}) copy-start(f32[1024,768]{1,0:T(8,128)} %fusion.10) | copy-start | bytes 9437188
  252.1 6.3 %copy-start.7 = (f32[1024,768]{1,0:T(8,128)S(1)}, f32[1024,768]{1,0:T(8,128)}, u32[]{:S(2)}) copy-start(f32[1024,768]{1,0:T(8,128)} %fusion.8) | copy-start | bytes 9437188
  252.1 14.8 %slice-start = ((s8[6291456]{0:T(1024)(128)(4,1)}), s8[4194304]{0:T(1024)(128)(4,1)S(1)}, s32[]{:S(2)}) async-start(s8[6291456]{0:T(1024)(128)(4,1)} %bitcast.126), calls=%async_computation.8 | async-start | bytes 8388608
  258.4 8.5 %slice-start.1 = ((s8[6291456]{0:T(1024)(128)(4,1)}), s8[2097152]{0:T(1024)(128)(4,1)S(1)}, s32[]{:S(2)}) async-start(s8[6291456]{0:T(1024)(128)(4,1)} %bitcast.126), calls=%async_computation.9 | async-start | bytes 4194304
  265.6 1.2 copy-start.8
  271.8 56.7 %all-to-all-start.3 = ((bf16[128,8,2048]{2,1,0:T(8,128)(2,1)}), bf16[128,8,2048]{2,1,0:T(8,128)(2,1)}, u32[]{:S(2)}, u32[]{:S(2)}) async-start(bf16[128,8,2048]{2,1,0:T(8,128)(2,1)} %convert_bitcast_fusion.1), calls=%async_computation.4 | async-start | bytes 8388608 | tf_op jit(solution)/shard_map/all_to_all | solution.py:169
  286.5 48.9 %copy-start.5 = (s32[1,128,4]{1,2,0:T(4,128)S(1)}, s32[1,128,4]{1,2,0:T(4,128)}, u32[]{:S(2)}) copy-start(s32[1,128,4]{1,2,0:T(4,128)} %param.25) | copy-start | bytes 6148
  328.5 56.7 %all-to-all-start.4 = ((bf16[128,8,2048]{2,1,0:T(8,128)(2,1)}), bf16[128,8,2048]{2,1,0:T(8,128)(2,1)}, u32[]{:S(2)}, u32[]{:S(2)}) async-start(bf16[128,8,2048]{2,1,0:T(8,128)(2,1)} %convert_bitcast_fusion), calls=%async_computation.5 | async-start | bytes 8388608 | tf_op jit(solution)/shard_map/all_to_all | solution.py:169
Sparse Core Ops, SparseCore 0:
  10.1 53.7 all-gather.1
  78.6 51.2 reduce-scatter.1

commit v2 on v1

--- a/solution.py
+++ b/solution.py
@@ -13,6 +13,7 @@
 HD = 128
 TOPK = 4
 CAP = 8
+PARTS = 2
 
 
 def attention_kernel(blocks, heads, width, buf_ref, out_ref, keys, values):
@@ -88,6 +89,45 @@
     )(buf)
 
 
+def retile_kernel(split, x_ref, out_ref):
+    half = D // 2
+    x = x_ref[...].astype(jnp.float32)
+    if split:
+        one, two = (x[:, at : at + half].reshape(-1, CAP, half) for at in (0, half))
+    else:
+        pairs = x.reshape(-1, 2 * CAP, half)
+        one, two = pairs[:, :CAP], pairs[:, CAP:]
+    upper = lax.broadcasted_iota(jnp.int32, one.shape, 1) < CAP // 2
+    if split:
+        first = jnp.where(upper, one, pltpu.roll(two, CAP // 2, 1))
+        second = jnp.where(upper, pltpu.roll(one, CAP // 2, 1), two)
+        out = jnp.concatenate([first, second], axis=1).reshape(-1, half)
+        out_ref[...] = out.astype(jnp.bfloat16)
+    else:
+        first = jnp.where(upper, one, pltpu.roll(two, CAP // 2, 1))
+        second = jnp.where(upper, pltpu.roll(one, CAP // 2, 1), two)
+        out_ref[:, :half] = first.reshape(-1, half).astype(jnp.bfloat16)
+        out_ref[:, half:] = second.reshape(-1, half).astype(jnp.bfloat16)
+
+
+def retile(x, split):
+    rows, columns = x.shape
+    shape = (rows * 2, columns // 2) if split else (rows // 2, columns * 2)
+    steps = math.gcd(8, max(rows, shape[0]) // (2 * CAP))
+    return pl.pallas_call(
+        functools.partial(retile_kernel, split),
+        grid=(steps,),
+        out_shape=jax.ShapeDtypeStruct(shape, jnp.bfloat16),
+        in_specs=[pl.BlockSpec((rows // steps, columns), lambda i: (i, 0))],
+        out_specs=pl.BlockSpec((shape[0] // steps, shape[1]), lambda i: (i, 0)),
+        compiler_params=pltpu.CompilerParams(vmem_limit_bytes=24 * 2**20),
+        cost_estimate=pl.CostEstimate(
+            flops=4 * rows * columns, transcendentals=0, bytes_accessed=4 * rows * columns
+        ),
+        name="retile_split" if split else "retile_join",
+    )(x)
+
+
 def per_device(
     hidden,
     queries,
@@ -136,44 +176,56 @@
     flat_ids = expert_ids[0].reshape(-1)
     one_hot = (flat_ids[:, None] == jnp.arange(experts, dtype=jnp.int32)[None, :]).astype(jnp.int32)
     earlier = jnp.cumsum(one_hot, axis=0) - one_hot
-    target = flat_ids * CAP + jnp.sum(earlier * one_hot, axis=1)
+    rank = jnp.sum(earlier * one_hot, axis=1)
+    target = (flat_ids * CAP + rank).reshape(rows, TOPK)
+    depth = CAP // 2
     slots = experts * CAP
-    hits = target.reshape(rows, TOPK)[:, :, None] == jnp.arange(slots, dtype=jnp.int32)
-    shares = gate_fixed[0][:, :, None]
-    high = jnp.sum(jnp.where(hits, shares // 256, 0), axis=1).astype(jnp.bfloat16)
-    low = jnp.sum(jnp.where(hits, shares % 256, 0), axis=1).astype(jnp.bfloat16)
-    pick = jnp.any(hits, axis=1).astype(jnp.bfloat16)
-
     half = D // 2
     exchange = functools.partial(
         lax.all_to_all, axis_name=("ctx", "exp"), split_axis=0, concat_axis=0, tiled=True
     )
-
-    def send(columns):
+    place = jnp.arange(slots, dtype=jnp.int32)
+    left = (place % CAP < depth)[None]
+    shares = gate_fixed[0][:, :, None]
+
+    def two_sides(array):
+        zero = jnp.zeros_like(array)
+        return jnp.concatenate([jnp.where(left, array, zero), jnp.where(left, zero, array)], axis=0)
+
+    def routing(part):
+        hits = target[:, :, None] == place // CAP * CAP + part * depth + place % depth
+        high = jnp.sum(jnp.where(hits, shares // 256, 0), axis=1)
+        low = jnp.sum(jnp.where(hits, shares % 256, 0), axis=1)
+        pick = jnp.any(hits, axis=1).astype(jnp.bfloat16)
+        gates = jnp.concatenate([high, low], axis=0).astype(jnp.bfloat16)
+        return two_sides(pick), two_sides(gates)
+
+    def send(pick):
+        sides = jnp.concatenate([normed[:, :half], normed[:, half:]], axis=0)
         rows_out = lax.dot_general(
-            pick, columns, (((0,), (0,)), ((), ())), preferred_element_type=jnp.float32
+            pick, sides, (((0,), (0,)), ((), ())), preferred_element_type=jnp.float32
         ).astype(jnp.bfloat16)
         return exchange(rows_out.reshape(experts, CAP, half)).reshape(slots, half)
 
-    first, second = send(normed[:, :half]), send(normed[:, half:])
-
-    def hidden_units(weight):
-        return jnp.dot(first, weight[:half], preferred_element_type=jnp.float32) + jnp.dot(
-            second, weight[half:], preferred_element_type=jnp.float32
+    def expert(arrived):
+        tokens = retile(arrived, False)
+        gate = jnp.dot(tokens, gate_proj[0], preferred_element_type=jnp.float32)
+        up = jnp.dot(tokens, up_proj[0], preferred_element_type=jnp.float32)
+        act = (jax.nn.silu(gate) * up).astype(jnp.bfloat16)
+        out = jnp.dot(act, down_proj[0], preferred_element_type=jnp.float32).astype(jnp.bfloat16)
+        tiles = retile(out, True)
+        return exchange(tiles.reshape(experts, CAP, half)).reshape(slots, half)
+
+    def combine(gates, back):
+        sides = jnp.dot(gates, back, preferred_element_type=jnp.float32).reshape(4, rows, half)
+        return jnp.concatenate(
+            [sides[at] * (1 / 256) + sides[at + 1] * (1 / 65536) for at in (0, 2)], axis=1
         )
 
-    act = (jax.nn.silu(hidden_units(gate_proj[0])) * hidden_units(up_proj[0])).astype(jnp.bfloat16)
-
-    def give_back(weight):
-        out = jnp.dot(act, weight, preferred_element_type=jnp.float32).astype(jnp.bfloat16)
-        back = exchange(out.reshape(experts, CAP, half)).reshape(slots, half)
-        return jnp.dot(high, back, preferred_element_type=jnp.float32) * (1 / 256) + jnp.dot(
-            low, back, preferred_element_type=jnp.float32
-        ) * (1 / 65536)
-
-    expert_sum = jnp.concatenate(
-        [give_back(down_proj[0][:, :half]), give_back(down_proj[0][:, half:])], axis=1
-    )
+    routes = [routing(part) for part in range(PARTS)]
+    arrived = [send(pick) for pick, _ in routes]
+    returned = [expert(tokens) for tokens in arrived]
+    expert_sum = sum(combine(gates, back) for (_, gates), back in zip(routes, returned))
     layer_output = (after_float + expert_sum).astype(jnp.bfloat16)
     return (after_attention[None], layer_output[None])
 

time: 405 us -> 383 us (0.946)
  waiting for transfers between devices: 218 us -> 169 us
  Pallas kernels: 25 us -> 37.5 us
  local copies, waits for them, and re-layouts: 7.65 us -> 19.7 us
    all_to_all x2, waiting for transfers between devices: 88.5 us -> 57.8 us  [expert(): return exchange(tiles.reshape(experts, CAP, half)).reshape(slots, half)]
    all_to_all x2, waiting for transfers between devices: 79.9 us -> 62 us  [send(): return exchange(rows_out.reshape(experts, CAP, half)).reshape(slots, half)]
    pallas_call x0 -> x4, Pallas kernels: none -> 12.4 us  [retile(): pl.pallas_call(functools.partial(retile_kernel, split), grid=(steps,), ou...]
    unnamed x25, local copies, waits for them, and re-layouts: 2.66 us -> 14.6 us
    dot_general x12 -> x8, matrix products: 61 us -> 60 us  [the longest x2 33.1 us: expert(): jnp.dot(act, down_proj[0], preferred_element_type=jnp.float32)]
  transfers between devices with their start and end apart: 6 -> 6, of which waited for: 5 -> 5; matrix products, arithmetic and copies ran while one was open for 9% -> 17% of each run, Pallas kernels for 6% -> 10%
where the time goes in v2:
time: 383 us; the launch traced here: 380 us
  waiting for transfers between devices  169 us (44%)
  matrix products  68.9 us (18%)
  Pallas kernels  37.5 us (10%)
  starting transfers between devices  31 us (8%)
  blocking collectives  30.7 us (8%)
  local copies, waits for them, and re-layouts  19.7 us (5%)
  between operations  14.4 us (4%)
  other arithmetic  8.43 us (2%)
    all_to_all x2, waiting for transfers between devices, send(): return exchange(rows_out.reshape(experts, CAP, half)).reshape(slots, half)  62 us
    all_to_all x2, waiting for transfers between devices, expert(): return exchange(tiles.reshape(experts, CAP, half)).reshape(slots, half)  57.8 us
    reduce_scatter x1, waiting for transfers between devices, per_device(): lax.psum_scatter(jnp.dot(attended, proj_rows, preferred_element_type=jnp....  48.7 us
    dot_general x2, matrix products, expert(): jnp.dot(act, down_proj[0], preferred_element_type=jnp.float32)  33.1 us
    all_to_all x1, blocking collectives, per_device(): lax.all_to_all(packed, 'ctx', split_axis=0, concat_axis=0, tiled=True)  30.7 us
    pallas_call x1, Pallas kernels, attention(): pl.pallas_call(functools.partial(attention_kernel, blocks, heads, min(512...  25 us
    all_to_all x2, starting transfers between devices, send(): return exchange(rows_out.reshape(experts, CAP, half)).reshape(slots, half)  17.2 us
    unnamed x25, local copies, waits for them, and re-layouts  14.6 us
  transfers between devices with their start and end apart: 6, of which 5 were waited for; matrix products, arithmetic and copies ran while one was open for 17% of the time, Pallas kernels for 10%

profile of v2, /device:TPU:12, one launch (start us, length us, event | category | flops | bytes accessed | tf_op | source)
XLA Modules:
  0.0 379.9 jit_solution(1567289213909794644)
XLA Ops:
  7.2 0.0 all-gather.2.cloned.1.call-start
  7.2 0.7 all-gather.2.cloned.1.call-update
  7.9 0.0 reduce-scatter.2.cloned.1.call-start
  7.9 0.9 reshape_squeeze.20
  8.9 0.9 reshape_squeeze.19
  9.8 0.9 reshape_squeeze.18
  10.8 0.9 reshape_squeeze.17
  11.7 0.3 pad_maximum_fusion.4
  12.0 0.1 copy.31
  12.1 1.6 copy.29
  13.8 0.5 copy.30
  14.3 0.1 broadcast_in_dim.87
  14.4 0.3 pad_maximum_fusion
  14.7 30.7 %all_to_all.25.buf_ref = bf16[8,128,1024]{2,1,0:T(8,128)(2,1)S(1)} all-to-all(bf16[8,128,1024]{2,1,0:T(8,128)(2,1)S(1)} %pad_maximum_fusion), channel_id=1, replica_groups=mesh['ctx'=8,'exp'=16] {'ctx'}, dimensions={0} | all-to-all | bytes 4194304 | tf_op jit(solution)/shard_map/all_to_all | solution.py:159
  45.4 25.0 %attention.1 = bf16[1024,512]{1,0:T(8,128)(2,1)S(1)} custom-call(bf16[8,128,1024]{2,1,0:T(8,128)(2,1)S(1)} %all_to_all.25.buf_ref), custom_call_target="tpu_custom_call" | custom-call | tf_op jit(solution)/shard_map/attention/pallas_call | solution.py:78
  70.4 0.0 all-gather.2.cloned.1.call-done
  70.4 8.9 %convolution_convert_fusion = bf16[1024,4096]{1,0:T(8,128)(2,1)} fusion(bf16[1024,512]{1,0:T(8,128)(2,1)S(1)} %attention.1, bf16[512,4096]{1,0:T(8,128)(2,1)} %all-gather.2.cloned.1.call-done), kind=kOutput, calls=%fused_computation | convolution fusion | flops 4299161600 | bytes 13631488 | tf_op jit(solution)/shard_map/dot_general | solution.py:163
  79.3 0.0 reduce-scatter.2.cloned.1.call-update
  79.4 0.7 copy-done.9
  80.0 0.1 copy.32
  80.1 0.1 eq.60
  80.2 0.1 eq.56
  80.4 0.1 copy.35
  80.5 0.2 fusion.58
  80.8 0.2 fusion.57
  81.0 0.1 reduce_sum.57
  81.2 0.1 copy.37
  81.3 0.7 compare_reduce_fusion.1
  82.0 0.1 convert_select_fusion.3
  82.1 48.7 %reduce-scatter.2.cloned.1.call-done = bf16[128,4096]{1,0:T(8,128)(2,1)} async-done(((bf16[1024,4096]{1,0:T(8,128)(2,1)}), bf16[128,4096]{1,0:T(8,128)(2,1)}) %reduce-scatter.2.cloned.1.call-update) | async-done | bytes 1048592 | tf_op jit(solution)/shard_map/reduce_scatter | solution.py:162
  130.8 1.7 fusion.22
  132.5 0.3 fusion.24
  132.8 0.1 fusion.85
  132.9 3.3 convert_bitcast_fusion
  136.2 10.3 %all-to-all-start.3 = ((bf16[128,8,2048]{2,1,0:T(8,128)(2,1)}), bf16[128,8,2048]{2,1,0:T(8,128)(2,1)}, u32[]{:S(2)}, u32[]{:S(2)}) async-start(bf16[128,8,2048]{2,1,0:T(8,128)(2,1)} %convert_bitcast_fusion), calls=%async_computation.4 | async-start | bytes 8388608 | tf_op jit(solution)/shard_map/all_to_all | solution.py:208
  146.6 3.2 convert_bitcast_fusion.1
  149.8 46.6 %all-to-all-done.3 = bf16[128,8,2048]{2,1,0:T(8,128)(2,1)} async-done(((bf16[128,8,2048]{2,1,0:T(8,128)(2,1)}), bf16[128,8,2048]{2,1,0:T(8,128)(2,1)}, u32[]{:S(2)}, u32[]{:S(2)}) %all-to-all-start.3) | async-done | bytes 4194336 | tf_op jit(solution)/shard_map/all_to_all | solution.py:208
  196.4 6.9 %all-to-all-start.1 = ((bf16[128,8,2048]{2,1,0:T(8,128)(2,1)}), bf16[128,8,2048]{2,1,0:T(8,128)(2,1)}, u32[]{:S(2)}, u32[]{:S(2)}) async-start(bf16[128,8,2048]{2,1,0:T(8,128)(2,1)} %convert_bitcast_fusion.1), calls=%async_computation.2 | async-start | bytes 8388608 | tf_op jit(solution)/shard_map/all_to_all | solution.py:208
  203.3 5.1 %retile_join.3 = bf16[512,4096]{1,0:T(8,128)(2,1)S(1)} custom-call(bf16[1024,2048]{1,0:T(8,128)(2,1)} %bitcast.22.x_ref), custom_call_target="tpu_custom_call" | custom-call | flops 8388608 | bytes 8388608 | tf_op jit(solution)/shard_map/retile_join/pallas_call | solution.py:117
  208.4 1.9 copy-done.2
  210.4 5.5 %fusion.8 = f32[512,768]{1,0:T(8,128)S(1)} fusion(bf16[512,4096]{1,0:T(8,128)(2,1)S(1)} %retile_join.3, bf16[1,4096,768]{2,1,0:T(8,128)(2,1)} %param.21), kind=kOutput, calls=%fused_computation.9 | convolution fusion | flops 3221225472 | bytes 12058624 | tf_op jit(solution)/shard_map/dot_general | solution.py:212
  215.9 16.6 %fusion.15.x_ref = bf16[512,4096]{1,0:T(8,128)(2,1)} fusion(bf16[1,768,4096]{2,1,0:T(8,128)(2,1)} %param.23, f32[512,768]{1,0:T(8,128)S(1)} %fusion.8, bf16[512,4096]{1,0:T(8,128)(2,1)} %copy-done.2, bf16[1,4096,768]{2,1,0:T(8,128)(2,1)} %param.22), kind=kOutput, calls=%fused_computation.14 | convolution fusion | flops 6446907392 | bytes 22544384 | tf_op jit(solution)/shard_map/dot_general | solution.py:215
  232.5 2.2 copy-done.3
  234.7 1.1 retile_split.3
  235.8 1.9 copy-done.1
  237.7 15.4 %all-to-all-done.1 = bf16[128,8,2048]{2,1,0:T(8,128)(2,1)} async-done(((bf16[128,8,2048]{2,1,0:T(8,128)(2,1)}), bf16[128,8,2048]{2,1,0:T(8,128)(2,1)}, u32[]{:S(2)}, u32[]{:S(2)}) %all-to-all-start.1) | async-done | bytes 4194336 | tf_op jit(solution)/shard_map/all_to_all | solution.py:208
  253.1 6.9 %all-to-all-start.4 = ((bf16[128,8,2048]{2,1,0:T(8,128)(2,1)}), bf16[128,8,2048]{2,1,0:T(8,128)(2,1)}, u32[]{:S(2)}, u32[]{:S(2)}) async-start(bf16[128,8,2048]{2,1,0:T(8,128)(2,1)} %bitcast.99), calls=%async_computation.5 | async-start | bytes 8388608 | tf_op jit(solution)/shard_map/all_to_all | solution.py:217
  260.0 5.1 %retile_join.2 = bf16[512,4096]{1,0:T(8,128)(2,1)S(1)} custom-call(bf16[1024,2048]{1,0:T(8,128)(2,1)} %bitcast.15.x_ref), custom_call_target="tpu_custom_call" | custom-call | flops 8388608 | bytes 8388608 | tf_op jit(solution)/shard_map/retile_join/pallas_call | solution.py:117
  265.1 2.0 copy-done.4
  267.1 5.5 %fusion.10 = f32[512,768]{1,0:T(8,128)S(1)} fusion(bf16[512,4096]{1,0:T(8,128)(2,1)S(1)} %retile_join.2, bf16[1,4096,768]{2,1,0:T(8,128)(2,1)} %param.21), kind=kOutput, calls=%fused_computation.11 | convolution fusion | flops 3221225472 | bytes 12058624 | tf_op jit(solution)/shard_map/dot_general | solution.py:212
  272.6 16.6 %fusion.12.x_ref = bf16[512,4096]{1,0:T(8,128)(2,1)} fusion(bf16[1,768,4096]{2,1,0:T(8,128)(2,1)} %param.23, f32[512,768]{1,0:T(8,128)S(1)} %fusion.10, bf16[512,4096]{1,0:T(8,128)(2,1)} %copy-done.4, bf16[1,4096,768]{2,1,0:T(8,128)(2,1)} %param.22), kind=kOutput, calls=%fused_computation.13 | convolution fusion | flops 6446907392 | bytes 22544384 | tf_op jit(solution)/shard_map/dot_general | solution.py:215
  289.2 2.2 copy-done.5
  291.4 1.1 retile_split.2
  292.4 2.0 copy-done
  294.4 15.4 %all-to-all-done.4 = bf16[128,8,2048]{2,1,0:T(8,128)(2,1)} async-done(((bf16[128,8,2048]{2,1,0:T(8,128)(2,1)}), bf16[128,8,2048]{2,1,0:T(8,128)(2,1)}, u32[]{:S(2)}, u32[]{:S(2)}) %all-to-all-start.4) | async-done | bytes 4194336 | tf_op jit(solution)/shard_map/all_to_all | solution.py:217
  309.8 6.9 %all-to-all-start.2 = ((bf16[128,8,2048]{2,1,0:T(8,128)(2,1)}), bf16[128,8,2048]{2,1,0:T(8,128)(2,1)}, u32[]{:S(2)}, u32[]{:S(2)}) async-start(bf16[128,8,2048]{2,1,0:T(8,128)(2,1)} %bitcast.98), calls=%async_computation.3 | async-start | bytes 8388608 | tf_op jit(solution)/shard_map/all_to_all | solution.py:217
  316.7 1.1 fusion.28
  318.0 1.3 broadcast_select_fusion.3
  319.3 4.5 %fusion.18 = f32[512,2048]{1,0:T(8,128)S(1)} fusion(bf16[128,8,2048]{2,1,0:T(8,128)(2,1)} %all-to-all-done.4, bf16[256,1024]{1,0:T(8,128)(2,1)S(1)} %get-tuple-element.28, bf16[256,1024]{1,0:T(8,128)(2,1)S(1)} %get-tuple-element.29), kind=kOutput, calls=%fused_computation.15 | convolution fusion | flops 2149580800 | bytes 9437184 | tf_op jit(solution)/shard_map/dot_general | solution.py:220
  323.9 0.3 fusion.37
  324.2 42.3 %all-to-all-done.2 = bf16[128,8,2048]{2,1,0:T(8,128)(2,1)} async-done(((bf16[128,8,2048]{2,1,0:T(8,128)(2,1)}), bf16[128,8,2048]{2,1,0:T(8,128)(2,1)}, u32[]{:S(2)}, u32[]{:S(2)}) %all-to-all-start.2) | async-done | bytes 4194336 | tf_op jit(solution)/shard_map/all_to_all | solution.py:217
  366.5 4.9 %fusion.20 = f32[512,2048]{1,0:T(8,128)S(1)} fusion(bf16[128,8,2048]{2,1,0:T(8,128)(2,1)} %all-to-all-done.2, bf16[256,1024]{1,0:T(8,128)(2,1)} %get-tuple-element.19, bf16[256,1024]{1,0:T(8,128)(2,1)} %get-tuple-element.18), kind=kOutput, calls=%fused_computation.17 | convolution fusion | flops 2149580800 | bytes 9437184 | tf_op jit(solution)/shard_map/dot_general | solution.py:220
  371.4 0.3 fusion.39
  371.7 1.3 fusion.35
  (31 shorter events, 0.3 us)
Async XLA Ops:
  7.2 63.3 %all-gather.2.cloned.1.call-start = ((), (), s32[]{:S(2)}) async-start(), calls=%async_computation.6 | async-start | bytes 4456448 | tf_op jit(solution)/shard_map/all_gather | solution.py:161
  7.9 122.9 %reduce-scatter.2.cloned.1.call-start = ((), (), s32[]{:S(2)}) async-start(), calls=%async_computation.7 | async-start | bytes 9437184 | tf_op jit(solution)/shard_map/reduce_scatter | solution.py:162
  79.3 0.7 copy-start.9
  79.3 1.0 copy-start.8
  79.3 51.5 %copy-start.7 = (bf16[1,128,4096]{2,1,0:T(8,128)(2,1)S(1)}, bf16[1,128,4096]{2,1,0:T(8,128)(2,1)}, u32[]{:S(2)}) copy-start(bf16[1,128,4096]{2,1,0:T(8,128)(2,1)} %param.13) | copy-start | bytes 3145732
  132.5 239.2 %copy-start.6 = (bf16[128,4096]{1,0:T(8,128)(2,1)}, bf16[128,4096]{1,0:T(8,128)(2,1)S(1)}, u32[]{:S(2)}) copy-start(bf16[128,4096]{1,0:T(8,128)(2,1)S(1)} %get-tuple-element.11) | copy-start | bytes 3145732
  136.2 60.2 %all-to-all-start.3 = ((bf16[128,8,2048]{2,1,0:T(8,128)(2,1)}), bf16[128,8,2048]{2,1,0:T(8,128)(2,1)}, u32[]{:S(2)}, u32[]{:S(2)}) async-start(bf16[128,8,2048]{2,1,0:T(8,128)(2,1)} %convert_bitcast_fusion), calls=%async_computation.4 | async-start | bytes 8388608 | tf_op jit(solution)/shard_map/all_to_all | solution.py:208
  196.4 56.7 %all-to-all-start.1 = ((bf16[128,8,2048]{2,1,0:T(8,128)(2,1)}), bf16[128,8,2048]{2,1,0:T(8,128)(2,1)}, u32[]{:S(2)}, u32[]{:S(2)}) async-start(bf16[128,8,2048]{2,1,0:T(8,128)(2,1)} %convert_bitcast_fusion.1), calls=%async_computation.2 | async-start | bytes 8388608 | tf_op jit(solution)/shard_map/all_to_all | solution.py:208
  208.4 2.0 copy-start.2
  232.5 2.2 copy-start.3
  235.7 2.0 copy-start.1
  253.1 56.7 %all-to-all-start.4 = ((bf16[128,8,2048]{2,1,0:T(8,128)(2,1)}), bf16[128,8,2048]{2,1,0:T(8,128)(2,1)}, u32[]{:S(2)}, u32[]{:S(2)}) async-start(bf16[128,8,2048]{2,1,0:T(8,128)(2,1)} %bitcast.99), calls=%async_computation.5 | async-start | bytes 8388608 | tf_op jit(solution)/shard_map/all_to_all | solution.py:217
  265.1 2.0 copy-start.4
  289.2 2.2 copy-start.5
  292.4 2.0 copy-start
  309.8 6.9 %copy-start.10 = (s32[1,128,4]{1,2,0:T(4,128)S(1)}, s32[1,128,4]{1,2,0:T(4,128)}, u32[]{:S(2)}) copy-start(s32[1,128,4]{1,2,0:T(4,128)} %param.25) | copy-start | bytes 6148
  309.8 56.7 %all-to-all-start.2 = ((bf16[128,8,2048]{2,1,0:T(8,128)(2,1)}), bf16[128,8,2048]{2,1,0:T(8,128)(2,1)}, u32[]{:S(2)}, u32[]{:S(2)}) async-start(bf16[128,8,2048]{2,1,0:T(8,128)(2,1)} %bitcast.98), calls=%async_computation.3 | async-start | bytes 8388608 | tf_op jit(solution)/shard_map/all_to_all | solution.py:217
Sparse Core Ops, SparseCore 0:
  10.1 53.7 all-gather.1
  79.5 51.2 reduce-scatter.1

commit v3 on v2

--- a/solution.py
+++ b/solution.py
@@ -128,6 +128,28 @@
     )(x)
 
 
+def pack_kernel(context, q_ref, ck_ref, nk_ref, cv_ref, nv_ref, out_ref):
+    base = q_ref.shape[1] // context
+    for c in range(context):
+        g = c // (context // KVH)
+        out_ref[c, :, :base] = q_ref[:, c * base : (c + 1) * base]
+        for k, ref in enumerate((ck_ref, nk_ref, cv_ref, nv_ref)):
+            at = base + k * HD
+            out_ref[c, :, at : at + HD] = ref[:, g * HD : (g + 1) * HD]
+
+
+def pack(context, *arrays):
+    rows, width = arrays[0].shape
+    return pl.pallas_call(
+        functools.partial(pack_kernel, context),
+        out_shape=jax.ShapeDtypeStruct((context, rows, width // context + 4 * HD), jnp.bfloat16),
+        in_specs=[pl.BlockSpec(memory_space=pltpu.VMEM)] * len(arrays),
+        out_specs=pl.BlockSpec(memory_space=pltpu.VMEM),
+        compiler_params=pltpu.CompilerParams(vmem_limit_bytes=16 * 2**20),
+        name="pack",
+    )(*arrays)
+
+
 def per_device(
     hidden,
     queries,
@@ -146,16 +168,11 @@
     context = lax.axis_size("ctx")
     experts = context * lax.axis_size("exp")
     rows = hidden.shape[1]
-    copies = context // KVH
     heads = queries.shape[2] // HD // context
 
-    def split(array, parts):
-        return jnp.swapaxes(array.reshape(rows, parts, -1), 0, 1)
-
-    kv = jnp.concatenate(
-        [split(a[0], KVH) for a in (cache_keys, new_keys, cache_values, new_values)], axis=2
+    packed = pack(
+        context, *(a[0] for a in (queries, cache_keys, new_keys, cache_values, new_values))
     )
-    packed = jnp.concatenate([split(queries[0], context), jnp.repeat(kv, copies, axis=0)], axis=2)
     received = lax.all_to_all(packed, "ctx", split_axis=0, concat_axis=0, tiled=True)
     attended = attention(received, heads)
     proj_rows = lax.all_gather(out_weight, "exp", axis=0, tiled=True)

time: 383 us -> 382 us (level)
    another operation x8 -> x3, local copies, waits for them, and re-layouts: 4.32 us -> 0.03 us  [the longest x5 4.3 us: split(): return jnp.swapaxes(array.reshape(rows, parts, -1), 0, 1)]
    unnamed x25 -> x34, local copies, waits for them, and re-layouts: 14.6 us -> 17.9 us
  transfers between devices with their start and end apart: 6 -> 6, of which waited for: 5 -> 5; matrix products, arithmetic and copies ran while one was open for 17% -> 15% of each run, Pallas kernels for 10% -> 10%
where the time goes in v3:
time: 382 us; the launch traced here: 378 us
  waiting for transfers between devices  169 us (44%)
  matrix products  68.9 us (18%)
  Pallas kernels  37.8 us (10%)
  starting transfers between devices  31.1 us (8%)
  blocking collectives  30.7 us (8%)
  local copies, waits for them, and re-layouts  18.5 us (5%)
  between operations  14.4 us (4%)
  other arithmetic  7.87 us (2%)
    all_to_all x2, waiting for transfers between devices, send(): return exchange(rows_out.reshape(experts, CAP, half)).reshape(slots, half)  62 us
    all_to_all x2, waiting for transfers between devices, expert(): return exchange(tiles.reshape(experts, CAP, half)).reshape(slots, half)  57.7 us
    reduce_scatter x1, waiting for transfers between devices, per_device(): lax.psum_scatter(jnp.dot(attended, proj_rows, preferred_element_type=jnp....  48.7 us
    dot_general x2, matrix products, expert(): jnp.dot(act, down_proj[0], preferred_element_type=jnp.float32)  33.1 us
    all_to_all x1, blocking collectives, per_device(): lax.all_to_all(packed, 'ctx', split_axis=0, concat_axis=0, tiled=True)  30.7 us
    pallas_call x1, Pallas kernels, attention(): pl.pallas_call(functools.partial(attention_kernel, blocks, heads, min(512...  25.1 us
    unnamed x34, local copies, waits for them, and re-layouts  17.9 us
    all_to_all x2, starting transfers between devices, send(): return exchange(rows_out.reshape(experts, CAP, half)).reshape(slots, half)  17.2 us
  transfers between devices with their start and end apart: 6, of which 5 were waited for; matrix products, arithmetic and copies ran while one was open for 15% of the time, Pallas kernels for 10%

profile of v3, /device:TPU:12, one launch (start us, length us, event | category | flops | bytes accessed | tf_op | source)
XLA Modules:
  0.0 378.4 jit_solution(1345453795077269374)
XLA Ops:
  7.2 0.0 all-gather.2.cloned.1.call-start
  7.2 0.7 all-gather.2.cloned.1.call-update
  7.9 0.0 reduce-scatter.2.cloned.1.call-start
  7.9 0.0 copy-start.6
  8.0 1.2 copy-done.6
  9.2 0.9 copy-done.7
  10.1 0.9 copy-done.8
  11.0 0.9 copy-done.9
  11.9 0.9 copy-done.10
  12.8 0.3 pack.1
  13.1 30.7 %all_to_all.25.buf_ref = bf16[8,128,1024]{2,1,0:T(8,128)(2,1)S(1)} all-to-all(bf16[8,128,1024]{2,1,0:T(8,128)(2,1)S(1)} %pack.1), channel_id=1, replica_groups=mesh['ctx'=8,'exp'=16] {'ctx'}, dimensions={0} | all-to-all | bytes 4194304 | tf_op jit(solution)/shard_map/all_to_all | solution.py:176
  43.8 25.1 %attention.1 = bf16[1024,512]{1,0:T(8,128)(2,1)S(1)} custom-call(bf16[8,128,1024]{2,1,0:T(8,128)(2,1)S(1)} %all_to_all.25.buf_ref), custom_call_target="tpu_custom_call" | custom-call | tf_op jit(solution)/shard_map/attention/pallas_call | solution.py:78
  68.9 0.0 all-gather.2.cloned.1.call-done
  68.9 8.9 %convolution_convert_fusion = bf16[1024,4096]{1,0:T(8,128)(2,1)} fusion(bf16[1024,512]{1,0:T(8,128)(2,1)S(1)} %attention.1, bf16[512,4096]{1,0:T(8,128)(2,1)} %all-gather.2.cloned.1.call-done), kind=kOutput, calls=%fused_computation | convolution fusion | flops 4299161600 | bytes 13631488 | tf_op jit(solution)/shard_map/dot_general | solution.py:180
  77.8 0.0 reduce-scatter.2.cloned.1.call-update
  77.8 0.7 copy-done.14
  78.5 0.1 copy.25
  78.6 0.1 eq.60
  78.7 0.1 eq.56
  78.8 0.1 copy.28
  79.0 0.2 fusion.58
  79.3 0.2 fusion.57
  79.5 0.1 reduce_sum.57
  79.6 0.1 copy.30
  79.7 0.7 compare_reduce_fusion.1
  80.5 0.1 convert_select_fusion.3
  80.6 48.7 %reduce-scatter.2.cloned.1.call-done = bf16[128,4096]{1,0:T(8,128)(2,1)} async-done(((bf16[1024,4096]{1,0:T(8,128)(2,1)}), bf16[128,4096]{1,0:T(8,128)(2,1)}) %reduce-scatter.2.cloned.1.call-update) | async-done | bytes 1048592 | tf_op jit(solution)/shard_map/reduce_scatter | solution.py:179
  129.3 1.7 fusion.22
  131.0 0.0 copy-start.11
  131.0 0.3 fusion.24
  131.3 0.1 fusion.85
  131.4 3.3 convert_bitcast_fusion
  134.7 10.4 %all-to-all-start.3 = ((bf16[128,8,2048]{2,1,0:T(8,128)(2,1)}), bf16[128,8,2048]{2,1,0:T(8,128)(2,1)}, u32[]{:S(2)}, u32[]{:S(2)}) async-start(bf16[128,8,2048]{2,1,0:T(8,128)(2,1)} %convert_bitcast_fusion), calls=%async_computation.4 | async-start | bytes 8388608 | tf_op jit(solution)/shard_map/all_to_all | solution.py:225
  145.1 3.2 convert_bitcast_fusion.1
  148.3 46.6 %all-to-all-done.3 = bf16[128,8,2048]{2,1,0:T(8,128)(2,1)} async-done(((bf16[128,8,2048]{2,1,0:T(8,128)(2,1)}), bf16[128,8,2048]{2,1,0:T(8,128)(2,1)}, u32[]{:S(2)}, u32[]{:S(2)}) %all-to-all-start.3) | async-done | bytes 4194336 | tf_op jit(solution)/shard_map/all_to_all | solution.py:225
  194.9 6.9 %all-to-all-start.1 = ((bf16[128,8,2048]{2,1,0:T(8,128)(2,1)}), bf16[128,8,2048]{2,1,0:T(8,128)(2,1)}, u32[]{:S(2)}, u32[]{:S(2)}) async-start(bf16[128,8,2048]{2,1,0:T(8,128)(2,1)} %convert_bitcast_fusion.1), calls=%async_computation.2 | async-start | bytes 8388608 | tf_op jit(solution)/shard_map/all_to_all | solution.py:225
  201.8 5.1 %retile_join.3 = bf16[512,4096]{1,0:T(8,128)(2,1)S(1)} custom-call(bf16[1024,2048]{1,0:T(8,128)(2,1)} %bitcast.20.x_ref), custom_call_target="tpu_custom_call" | custom-call | flops 8388608 | bytes 8388608 | tf_op jit(solution)/shard_map/retile_join/pallas_call | solution.py:117
  206.9 2.0 copy-done.2
  208.9 5.5 %fusion.8 = f32[512,768]{1,0:T(8,128)S(1)} fusion(bf16[512,4096]{1,0:T(8,128)(2,1)S(1)} %retile_join.3, bf16[1,4096,768]{2,1,0:T(8,128)(2,1)} %param.21), kind=kOutput, calls=%fused_computation.9 | convolution fusion | flops 3221225472 | bytes 12058624 | tf_op jit(solution)/shard_map/dot_general | solution.py:229
  214.4 16.6 %fusion.15.x_ref = bf16[512,4096]{1,0:T(8,128)(2,1)} fusion(bf16[1,768,4096]{2,1,0:T(8,128)(2,1)} %param.23, f32[512,768]{1,0:T(8,128)S(1)} %fusion.8, bf16[512,4096]{1,0:T(8,128)(2,1)} %copy-done.2, bf16[1,4096,768]{2,1,0:T(8,128)(2,1)} %param.22), kind=kOutput, calls=%fused_computation.14 | convolution fusion | flops 6446907392 | bytes 22544384 | tf_op jit(solution)/shard_map/dot_general | solution.py:232
  231.0 2.2 copy-done.3
  233.2 1.1 retile_split.3
  234.3 2.0 copy-done.1
  236.2 15.4 %all-to-all-done.1 = bf16[128,8,2048]{2,1,0:T(8,128)(2,1)} async-done(((bf16[128,8,2048]{2,1,0:T(8,128)(2,1)}), bf16[128,8,2048]{2,1,0:T(8,128)(2,1)}, u32[]{:S(2)}, u32[]{:S(2)}) %all-to-all-start.1) | async-done | bytes 4194336 | tf_op jit(solution)/shard_map/all_to_all | solution.py:225
  251.6 6.9 %all-to-all-start.4 = ((bf16[128,8,2048]{2,1,0:T(8,128)(2,1)}), bf16[128,8,2048]{2,1,0:T(8,128)(2,1)}, u32[]{:S(2)}, u32[]{:S(2)}) async-start(bf16[128,8,2048]{2,1,0:T(8,128)(2,1)} %bitcast.97), calls=%async_computation.5 | async-start | bytes 8388608 | tf_op jit(solution)/shard_map/all_to_all | solution.py:234
  258.5 5.1 %retile_join.2 = bf16[512,4096]{1,0:T(8,128)(2,1)S(1)} custom-call(bf16[1024,2048]{1,0:T(8,128)(2,1)} %bitcast.13.x_ref), custom_call_target="tpu_custom_call" | custom-call | flops 8388608 | bytes 8388608 | tf_op jit(solution)/shard_map/retile_join/pallas_call | solution.py:117
  263.6 0.0 copy-start.4
  263.7 2.0 copy-done.4
  265.6 5.5 %fusion.10 = f32[512,768]{1,0:T(8,128)S(1)} fusion(bf16[512,4096]{1,0:T(8,128)(2,1)S(1)} %retile_join.2, bf16[1,4096,768]{2,1,0:T(8,128)(2,1)} %param.21), kind=kOutput, calls=%fused_computation.11 | convolution fusion | flops 3221225472 | bytes 12058624 | tf_op jit(solution)/shard_map/dot_general | solution.py:229
  271.1 16.6 %fusion.12.x_ref = bf16[512,4096]{1,0:T(8,128)(2,1)} fusion(bf16[1,768,4096]{2,1,0:T(8,128)(2,1)} %param.23, f32[512,768]{1,0:T(8,128)S(1)} %fusion.10, bf16[512,4096]{1,0:T(8,128)(2,1)} %copy-done.4, bf16[1,4096,768]{2,1,0:T(8,128)(2,1)} %param.22), kind=kOutput, calls=%fused_computation.13 | convolution fusion | flops 6446907392 | bytes 22544384 | tf_op jit(solution)/shard_map/dot_general | solution.py:232
  287.7 2.2 copy-done.5
  289.9 1.1 retile_split.2
  290.9 0.0 copy-start
  291.0 2.0 copy-done
  292.9 15.4 %all-to-all-done.4 = bf16[128,8,2048]{2,1,0:T(8,128)(2,1)} async-done(((bf16[128,8,2048]{2,1,0:T(8,128)(2,1)}), bf16[128,8,2048]{2,1,0:T(8,128)(2,1)}, u32[]{:S(2)}, u32[]{:S(2)}) %all-to-all-start.4) | async-done | bytes 4194336 | tf_op jit(solution)/shard_map/all_to_all | solution.py:234
  308.3 6.9 %all-to-all-start.2 = ((bf16[128,8,2048]{2,1,0:T(8,128)(2,1)}), bf16[128,8,2048]{2,1,0:T(8,128)(2,1)}, u32[]{:S(2)}, u32[]{:S(2)}) async-start(bf16[128,8,2048]{2,1,0:T(8,128)(2,1)} %bitcast.96), calls=%async_computation.3 | async-start | bytes 8388608 | tf_op jit(solution)/shard_map/all_to_all | solution.py:234
  315.2 1.1 fusion.28
  316.5 1.3 broadcast_select_fusion.3
  317.9 4.5 %fusion.18 = f32[512,2048]{1,0:T(8,128)S(1)} fusion(bf16[128,8,2048]{2,1,0:T(8,128)(2,1)} %all-to-all-done.4, bf16[256,1024]{1,0:T(8,128)(2,1)S(1)} %get-tuple-element.28, bf16[256,1024]{1,0:T(8,128)(2,1)S(1)} %get-tuple-element.29), kind=kOutput, calls=%fused_computation.15 | convolution fusion | flops 2149580800 | bytes 9437184 | tf_op jit(solution)/shard_map/dot_general | solution.py:237
  322.4 0.3 fusion.37
  322.7 42.3 %all-to-all-done.2 = bf16[128,8,2048]{2,1,0:T(8,128)(2,1)} async-done(((bf16[128,8,2048]{2,1,0:T(8,128)(2,1)}), bf16[128,8,2048]{2,1,0:T(8,128)(2,1)}, u32[]{:S(2)}, u32[]{:S(2)}) %all-to-all-start.2) | async-done | bytes 4194336 | tf_op jit(solution)/shard_map/all_to_all | solution.py:234
  365.0 4.9 %fusion.20 = f32[512,2048]{1,0:T(8,128)S(1)} fusion(bf16[128,8,2048]{2,1,0:T(8,128)(2,1)} %all-to-all-done.2, bf16[256,1024]{1,0:T(8,128)(2,1)} %get-tuple-element.19, bf16[256,1024]{1,0:T(8,128)(2,1)} %get-tuple-element.18), kind=kOutput, calls=%fused_computation.17 | convolution fusion | flops 2149580800 | bytes 9437184 | tf_op jit(solution)/shard_map/dot_general | solution.py:237
  369.9 0.3 fusion.39
  370.2 1.3 fusion.35
  (32 shorter events, 0.3 us)
Async XLA Ops:
  7.2 61.7 %all-gather.2.cloned.1.call-start = ((), (), s32[]{:S(2)}) async-start(), calls=%async_computation.6 | async-start | bytes 4456448 | tf_op jit(solution)/shard_map/all_gather | solution.py:178
  7.9 121.4 %reduce-scatter.2.cloned.1.call-start = ((), (), s32[]{:S(2)}) async-start(), calls=%async_computation.7 | async-start | bytes 9437184 | tf_op jit(solution)/shard_map/reduce_scatter | solution.py:179
  7.9 1.2 copy-start.6
  9.2 0.9 copy-start.7
  10.1 0.9 copy-start.8
  11.0 0.9 copy-start.9
  11.9 0.9 copy-start.10
  77.8 0.7 copy-start.14
  77.8 1.0 copy-start.13
  77.8 51.5 %copy-start.12 = (bf16[1,128,4096]{2,1,0:T(8,128)(2,1)S(1)}, bf16[1,128,4096]{2,1,0:T(8,128)(2,1)}, u32[]{:S(2)}) copy-start(bf16[1,128,4096]{2,1,0:T(8,128)(2,1)} %param.13) | copy-start | bytes 3145732
  131.0 239.3 %copy-start.11 = (bf16[128,4096]{1,0:T(8,128)(2,1)}, bf16[128,4096]{1,0:T(8,128)(2,1)S(1)}, u32[]{:S(2)}) copy-start(bf16[128,4096]{1,0:T(8,128)(2,1)S(1)} %get-tuple-element.11) | copy-start | bytes 3145732
  134.7 60.2 %all-to-all-start.3 = ((bf16[128,8,2048]{2,1,0:T(8,128)(2,1)}), bf16[128,8,2048]{2,1,0:T(8,128)(2,1)}, u32[]{:S(2)}, u32[]{:S(2)}) async-start(bf16[128,8,2048]{2,1,0:T(8,128)(2,1)} %convert_bitcast_fusion), calls=%async_computation.4 | async-start | bytes 8388608 | tf_op jit(solution)/shard_map/all_to_all | solution.py:225
  194.9 56.7 %all-to-all-start.1 = ((bf16[128,8,2048]{2,1,0:T(8,128)(2,1)}), bf16[128,8,2048]{2,1,0:T(8,128)(2,1)}, u32[]{:S(2)}, u32[]{:S(2)}) async-start(bf16[128,8,2048]{2,1,0:T(8,128)(2,1)} %convert_bitcast_fusion.1), calls=%async_computation.2 | async-start | bytes 8388608 | tf_op jit(solution)/shard_map/all_to_all | solution.py:225
  206.9 2.0 copy-start.2
  231.0 2.2 copy-start.3
  234.3 2.0 copy-start.1
  251.6 56.7 %all-to-all-start.4 = ((bf16[128,8,2048]{2,1,0:T(8,128)(2,1)}), bf16[128,8,2048]{2,1,0:T(8,128)(2,1)}, u32[]{:S(2)}, u32[]{:S(2)}) async-start(bf16[128,8,2048]{2,1,0:T(8,128)(2,1)} %bitcast.97), calls=%async_computation.5 | async-start | bytes 8388608 | tf_op jit(solution)/shard_map/all_to_all | solution.py:234
  263.6 2.0 copy-start.4
  287.7 2.2 copy-start.5
  290.9 2.0 copy-start
  308.3 6.9 %copy-start.15 = (s32[1,128,4]{1,2,0:T(4,128)S(1)}, s32[1,128,4]{1,2,0:T(4,128)}, u32[]{:S(2)}) copy-start(s32[1,128,4]{1,2,0:T(4,128)} %param.25) | copy-start | bytes 6148
  308.3 56.7 %all-to-all-start.2 = ((bf16[128,8,2048]{2,1,0:T(8,128)(2,1)}), bf16[128,8,2048]{2,1,0:T(8,128)(2,1)}, u32[]{:S(2)}, u32[]{:S(2)}) async-start(bf16[128,8,2048]{2,1,0:T(8,128)(2,1)} %bitcast.96), calls=%async_computation.3 | async-start | bytes 8388608 | tf_op jit(solution)/shard_map/all_to_all | solution.py:234
Sparse Core Ops, SparseCore 0:
  10.1 53.6 all-gather.1
  78.0 51.2 reduce-scatter.1
